TPU v7x, 32 devices: a whole 2x2x4 slice. The times are simulated.
32 devices in a mesh: dp: 16 (over z, y, x), tensor: 2 (over core).
Axes of the slice: x: 2, y: 2, z: 4, core: 2. Of those that a mesh axis runs over, the one named last changes fastest.
Arguments:
- tokens: bfloat16 [16384, 1024], P('dp'), may hold values from -6 to 6
- cotangent: bfloat16 [16384, 1024], P('dp'), may hold values from -6 to 6
- segment_ids: int32 [32, 512], P('dp'), may hold values from 0 to 5, never falling along the last dimension, each value on 1 to 200 neighbouring positions
- adapter_ids: int32 [32], P('dp'), may hold values from 0 to 7, as said below
- query_weight: bfloat16 [1024, 1024], P(None, 'tensor'), may hold values from -0.1875 to 0.1875
- key_weight: bfloat16 [1024, 1024], P(None, 'tensor'), may hold values from -0.1875 to 0.1875
- value_weight: bfloat16 [1024, 1024], P(None, 'tensor'), may hold values from -0.1875 to 0.1875
- output_weight: bfloat16 [1024, 1024], P('tensor'), may hold values from -0.75 to 0.75
- expand_weight: bfloat16 [1024, 4096], P(None, 'tensor'), may hold values from -0.1875 to 0.1875
- contract_weight: bfloat16 [4096, 1024], P('tensor'), may hold values from -0.09375 to 0.09375
- first_gain: float32 [1024], replicated, may hold values from 0.5 to 1.5
- first_shift: float32 [1024], replicated, may hold values from -3 to 3
- second_gain: float32 [1024], replicated, may hold values from 0.5 to 1.5
- second_shift: float32 [1024], replicated, may hold values from -3 to 3
- query_down: bfloat16 [8, 1024, 16], replicated, may hold values from -0.1875 to 0.1875
- query_up: bfloat16 [8, 16, 1024], P(None, None, 'tensor'), may hold values from -1.5 to 1.5
- key_down: bfloat16 [8, 1024, 16], replicated, may hold values from -0.1875 to 0.1875
- key_up: bfloat16 [8, 16, 1024], P(None, None, 'tensor'), may hold values from -1.5 to 1.5
- value_down: bfloat16 [8, 1024, 16], replicated, may hold values from -0.1875 to 0.1875
- value_up: bfloat16 [8, 16, 1024], P(None, None, 'tensor'), may hold values from -1.5 to 1.5
- output_down: bfloat16 [8, 1024, 16], P(None, 'tensor'), may hold values from -0.75 to 0.75
- output_up: bfloat16 [8, 16, 1024], replicated, may hold values from -1.5 to 1.5
- expand_down: bfloat16 [8, 1024, 16], replicated, may hold values from -0.1875 to 0.1875
- expand_up: bfloat16 [8, 16, 4096], P(None, None, 'tensor'), may hold values from -1.5 to 1.5
- contract_down: bfloat16 [8, 4096, 16], P(None, 'tensor'), may hold values from -0.09375 to 0.09375
- contract_up: bfloat16 [8, 16, 1024], replicated, may hold values from -1.5 to 1.5
Outputs:
- layer_output: bfloat16 [16384, 1024], P('dp')
- input_gradient: bfloat16 [16384, 1024], P('dp')
- gradient_query_down: float32 [8, 1024, 16], replicated
- gradient_query_up: float32 [8, 16, 1024], P(None, None, 'tensor')
- gradient_key_down: float32 [8, 1024, 16], replicated
- gradient_key_up: float32 [8, 16, 1024], P(None, None, 'tensor')
- gradient_value_down: float32 [8, 1024, 16], replicated
- gradient_value_up: float32 [8, 16, 1024], P(None, None, 'tensor')
- gradient_output_down: float32 [8, 1024, 16], P(None, 'tensor')
- gradient_output_up: float32 [8, 16, 1024], replicated
- gradient_expand_down: float32 [8, 1024, 16], replicated
- gradient_expand_up: float32 [8, 16, 4096], P(None, None, 'tensor')
- gradient_contract_down: float32 [8, 4096, 16], P(None, 'tensor')
- gradient_contract_up: float32 [8, 16, 1024], replicated
Inputs may be any that keep to these rules, and one draw needn't show every extreme that they name: `adapter_ids`: each of the 8 adapters serves 32 // 8 sequences or one more. `segment_ids`: numbers never fall along a sequence; every sequence holds 6 documents of 1 to 200 tokens, one of exactly 200.
All inputs are finite; a program needn't handle non-finite values.
Results may differ from a plain program's by a relative error of at most 0.019.
Values sent between devices are 32-bit elements; how exact they have to be, the bound alone decides.
A program may use at most 192 MiB of HBM per device.

v0:
```python
import jax
import jax.numpy as jnp
from jax import lax
from jax.sharding import PartitionSpec as P

HEAD_WIDTH = 64


FULL_PRECISION = lax.Precision.HIGHEST
epsilon = 1e-05


def select_table(adapter_selector, table):
    return jnp.einsum(
        "se,eab->sab", adapter_selector, table, preferred_element_type=jnp.float32
    ).astype(jnp.bfloat16)


def spread(adapter_selector, per_sequence):
    return jnp.einsum(
        "se,sab->eab", adapter_selector.astype(jnp.float32), per_sequence, precision=FULL_PRECISION
    )


def mixed(form, left, right):
    return jnp.einsum(
        form, left.astype(jnp.float32), right.astype(jnp.float32), precision=FULL_PRECISION
    )


def low_rank(input_activation, down_projection_table):
    return jnp.einsum(
        "qxm,qmw->qxw", input_activation, down_projection_table, preferred_element_type=jnp.float32
    )


def lift_rank(rank_space_rows, up_table):
    return jnp.einsum("slr,srn->sln", rank_space_rows, up_table, preferred_element_type=jnp.float32)


def project(input_activation, dense_weight):
    return jnp.einsum(
        "bhp,pz->bhz", input_activation, dense_weight, preferred_element_type=jnp.float32
    )


def project_back(gradient_token_rows, dense_weight):
    return jnp.einsum(
        "zpi,hi->zph", gradient_token_rows, dense_weight, preferred_element_type=jnp.float32
    )


def rank_back(gradient_token_rows, up_table):
    return jnp.einsum(
        "sln,srn->slr", gradient_token_rows, up_table, preferred_element_type=jnp.float32
    )


def down_back(rank_space_gradient, down_projection_table):
    return jnp.einsum(
        "kyg,kxg->kyx",
        rank_space_gradient,
        down_projection_table,
        preferred_element_type=jnp.float32,
    )


def outer_grad(left_rows, right_rows):
    return jnp.einsum("sla,slb->sab", left_rows, right_rows, preferred_element_type=jnp.float32)


def layer_norm(summed, norm_gain, norm_shift):
    average = jnp.mean(summed, axis=-1, keepdims=True)
    centered = summed - average
    variance = jnp.mean(centered * centered, axis=-1, keepdims=True)
    return centered * lax.rsqrt(variance + epsilon) * norm_gain + norm_shift


def gelu_exact(value):
    return jax.nn.gelu(value, approximate=False)


def masked_scores(query_matrix, key_token_rows, segment):
    attention_logits = jnp.einsum(
        "ayb,oyb->yao", query_matrix, key_token_rows, preferred_element_type=jnp.float32
    ) * HEAD_WIDTH ** (-0.5)
    same_doc = segment[:, None] == segment[None, :]
    return jnp.where(same_doc[None, :, :], attention_logits, -1e30)


def forward_one(bundle):
    query_matrix, key_token_rows, value_matrix, segment = bundle
    attention_logits = masked_scores(query_matrix, key_token_rows, segment)
    row_max = jnp.max(attention_logits, axis=-1, keepdims=True)
    exponent = jnp.exp(attention_logits - row_max)
    row_total = jnp.sum(exponent, axis=-1, keepdims=True)
    weight_bundle = (exponent / row_total).astype(jnp.bfloat16)
    blended_heads = jnp.einsum(
        "jop,pjc->ojc", weight_bundle, value_matrix, preferred_element_type=jnp.float32
    ).astype(jnp.bfloat16)
    return (blended_heads, (row_max + jnp.log(row_total))[:, :, 0])


def backward_one(bundle):
    query_matrix, key_token_rows, value_matrix, segment, log_total, output_cotangent = bundle
    attention_logits = masked_scores(query_matrix, key_token_rows, segment)
    attention_probabilities = jnp.exp(attention_logits - log_total[:, :, None])
    probability_gradient = jnp.einsum(
        "ayb,oyb->yao", output_cotangent, value_matrix, preferred_element_type=jnp.float32
    )
    row_dot = jnp.sum(attention_probabilities * probability_gradient, axis=-1, keepdims=True)
    score_gradient = (attention_probabilities * (probability_gradient - row_dot)).astype(
        jnp.bfloat16
    )
    score_scale = HEAD_WIDTH ** (-0.5)
    back_query = (
        jnp.einsum(
            "jop,pjc->ojc", score_gradient, key_token_rows, preferred_element_type=jnp.float32
        )
        * score_scale
    ).astype(jnp.bfloat16)
    back_key = (
        jnp.einsum("yxw,xyc->wyc", score_gradient, query_matrix, preferred_element_type=jnp.float32)
        * score_scale
    ).astype(jnp.bfloat16)
    back_value = jnp.einsum(
        "yxw,xyc->wyc",
        attention_probabilities.astype(jnp.bfloat16),
        output_cotangent,
        preferred_element_type=jnp.float32,
    ).astype(jnp.bfloat16)
    return (back_query, back_key, back_value)


def on_device(
    tokens,
    cotangent,
    segment_ids,
    adapter_ids,
    query_weight,
    key_weight,
    value_weight,
    output_weight,
    expand_weight,
    contract_weight,
    first_gain,
    first_shift,
    second_gain,
    second_shift,
    query_down,
    query_up,
    key_down,
    key_up,
    value_down,
    value_up,
    output_down,
    output_up,
    expand_down,
    expand_up,
    contract_down,
    contract_up,
):
    seq_count = adapter_ids.shape[0]
    length = segment_ids.shape[1]
    model_width = tokens.shape[1]
    head_count = query_weight.shape[1] // HEAD_WIDTH
    adapter_selector = (
        adapter_ids[:, None] == jnp.arange(query_down.shape[0], dtype=jnp.int32)[None, :]
    ).astype(jnp.bfloat16)
    token_rows = tokens.reshape(seq_count, length, model_width)
    query_lower = select_table(adapter_selector, query_down)
    query_upper = select_table(adapter_selector, query_up)
    key_lower = select_table(adapter_selector, key_down)
    key_upper = select_table(adapter_selector, key_up)
    value_lower = select_table(adapter_selector, value_down)
    value_upper = select_table(adapter_selector, value_up)
    output_lower = select_table(adapter_selector, output_down)
    output_upper = select_table(adapter_selector, output_up)
    expand_lower = select_table(adapter_selector, expand_down)
    expand_upper = select_table(adapter_selector, expand_up)
    contract_lower = select_table(adapter_selector, contract_down)
    contract_upper = select_table(adapter_selector, contract_up)

    def attention_inputs(dense_weight, lower_table, upper_table):
        rank_space_rows = low_rank(token_rows, lower_table).astype(jnp.bfloat16)
        projected = (
            project(token_rows, dense_weight) + lift_rank(rank_space_rows, upper_table)
        ).astype(jnp.bfloat16)
        return (rank_space_rows, projected)

    query_rank, query_matrix = attention_inputs(query_weight, query_lower, query_upper)
    key_rank, key_token_rows = attention_inputs(key_weight, key_lower, key_upper)
    value_rank, value_matrix = attention_inputs(value_weight, value_lower, value_upper)
    shape_heads = (seq_count, length, head_count, HEAD_WIDTH)
    query_heads = query_matrix.reshape(shape_heads)
    key_heads = key_token_rows.reshape(shape_heads)
    value_heads = value_matrix.reshape(shape_heads)
    head_out, log_total = lax.map(forward_one, (query_heads, key_heads, value_heads, segment_ids))
    head_flat = head_out.reshape(seq_count, length, head_count * HEAD_WIDTH)
    branch_main, output_rank = lax.psum(
        (project(head_flat, output_weight), low_rank(head_flat, output_lower)), "tensor"
    )
    branch = branch_main + mixed("slr,srn->sln", output_rank, output_upper)
    normed, first_back = jax.vjp(
        lambda summed: layer_norm(summed, first_gain, first_shift),
        token_rows.astype(jnp.float32) + branch,
    )
    inner_in = normed.astype(jnp.bfloat16)
    expand_rank = low_rank(inner_in, expand_lower).astype(jnp.bfloat16)
    before = project(inner_in, expand_weight) + lift_rank(expand_rank, expand_upper)
    activated, gelu_back = jax.vjp(gelu_exact, before)
    hidden = activated.astype(jnp.bfloat16)
    outer_main, contract_rank = lax.psum(
        (project(hidden, contract_weight), low_rank(hidden, contract_lower)), "tensor"
    )
    outer_sum = outer_main + mixed("slr,srn->sln", contract_rank, contract_upper)
    result, second_back = jax.vjp(
        lambda summed: layer_norm(summed, second_gain, second_shift), normed + outer_sum
    )
    layer_output = result.reshape(seq_count * length, model_width).astype(jnp.bfloat16)
    back_second = second_back(
        cotangent.astype(jnp.float32).reshape(seq_count, length, model_width)
    )[0]
    back_outer = back_second.astype(jnp.bfloat16)
    term_contract_up = mixed("sla,slb->sab", contract_rank, back_outer)
    back_contract_rank = rank_back(back_outer, contract_upper).astype(jnp.bfloat16)
    term_contract_down = outer_grad(hidden, back_contract_rank)
    back_hidden = project_back(back_outer, contract_weight) + down_back(
        back_contract_rank, contract_lower
    )
    back_before = gelu_back(back_hidden)[0].astype(jnp.bfloat16)
    term_expand_up = outer_grad(expand_rank, back_before)
    back_inner, back_expand_rank = lax.psum(
        (project_back(back_before, expand_weight), rank_back(back_before, expand_upper)), "tensor"
    )
    term_expand_down = mixed("sla,slb->sab", inner_in, back_expand_rank)
    back_normed = back_second + back_inner + mixed("kyg,kxg->kyx", back_expand_rank, expand_lower)
    back_first = first_back(back_normed)[0]
    expand_parts = (
        spread(adapter_selector, term_expand_down),
        spread(adapter_selector, term_expand_up),
        spread(adapter_selector, term_contract_down),
        spread(adapter_selector, term_contract_up),
    )
    back_branch = back_first.astype(jnp.bfloat16)
    term_output_up = mixed("sla,slb->sab", output_rank, back_branch)
    back_output_rank = rank_back(back_branch, output_upper).astype(jnp.bfloat16)
    term_output_down = outer_grad(head_flat, back_output_rank)
    back_heads = (
        project_back(back_branch, output_weight) + down_back(back_output_rank, output_lower)
    ).astype(jnp.bfloat16)
    back_query, back_key, back_value = lax.map(
        backward_one,
        (
            query_heads,
            key_heads,
            value_heads,
            segment_ids,
            log_total,
            back_heads.reshape(shape_heads),
        ),
    )
    flat_shape = (seq_count, length, head_count * HEAD_WIDTH)
    back_query = back_query.reshape(flat_shape)
    back_key = back_key.reshape(flat_shape)
    back_value = back_value.reshape(flat_shape)
    term_query_up = outer_grad(query_rank, back_query)
    term_key_up = outer_grad(key_rank, back_key)
    term_value_up = outer_grad(value_rank, back_value)
    back_partial = (
        project_back(back_query, query_weight)
        + project_back(back_key, key_weight)
        + project_back(back_value, value_weight)
    )
    back_projected, back_query_rank, back_key_rank, back_value_rank = lax.psum(
        (
            back_partial,
            rank_back(back_query, query_upper),
            rank_back(back_key, key_upper),
            rank_back(back_value, value_upper),
        ),
        "tensor",
    )
    term_query_down = mixed("sla,slb->sab", token_rows, back_query_rank)
    term_key_down = mixed("sla,slb->sab", token_rows, back_key_rank)
    term_value_down = mixed("sla,slb->sab", token_rows, back_value_rank)
    input_total = (
        back_first
        + back_projected
        + mixed("kyg,kxg->kyx", back_query_rank, query_lower)
        + mixed("kyg,kxg->kyx", back_key_rank, key_lower)
        + mixed("kyg,kxg->kyx", back_value_rank, value_lower)
    )
    input_gradient = input_total.reshape(seq_count * length, model_width).astype(jnp.bfloat16)
    attention_parts = (
        spread(adapter_selector, term_query_down),
        spread(adapter_selector, term_query_up),
        spread(adapter_selector, term_key_down),
        spread(adapter_selector, term_key_up),
        spread(adapter_selector, term_value_down),
        spread(adapter_selector, term_value_up),
        spread(adapter_selector, term_output_down),
        spread(adapter_selector, term_output_up),
    )
    summed_parts = lax.psum(
        (
            attention_parts[0],
            attention_parts[1],
            attention_parts[2],
            attention_parts[3],
            attention_parts[4],
            attention_parts[5],
            attention_parts[6],
            attention_parts[7],
            expand_parts[0],
            expand_parts[1],
            expand_parts[2],
            expand_parts[3],
        ),
        "dp",
    )
    attention_parts = summed_parts[0:8]
    expand_parts = summed_parts[8:12]
    return (
        layer_output,
        input_gradient,
        attention_parts[0],
        attention_parts[1],
        attention_parts[2],
        attention_parts[3],
        attention_parts[4],
        attention_parts[5],
        attention_parts[6],
        attention_parts[7],
        expand_parts[0],
        expand_parts[1],
        expand_parts[2],
        expand_parts[3],
    )


def solution(mesh):
    return jax.shard_map(
        on_device,
        mesh=mesh,
        in_specs=(
            P("dp", None),
            P("dp", None),
            P("dp", None),
            P("dp"),
            P(None, "tensor"),
            P(None, "tensor"),
            P(None, "tensor"),
            P("tensor", None),
            P(None, "tensor"),
            P("tensor", None),
            P(),
            P(),
            P(),
            P(),
            P(),
            P(None, None, "tensor"),
            P(),
            P(None, None, "tensor"),
            P(),
            P(None, None, "tensor"),
            P(None, "tensor", None),
            P(),
            P(),
            P(None, None, "tensor"),
            P(None, "tensor", None),
            P(),
        ),
        out_specs=(
            P("dp", None),
            P("dp", None),
            P(),
            P(None, None, "tensor"),
            P(),
            P(None, None, "tensor"),
            P(),
            P(None, None, "tensor"),
            P(None, "tensor", None),
            P(),
            P(),
            P(None, None, "tensor"),
            P(None, "tensor", None),
            P(),
        ),
        check_vma=False,
    )
```

profile of v0, /device:TPU:0, one launch (start us, length us, event | category | flops | bytes accessed | tf_op | source)
XLA Modules:
  0.0 571.7 jit_solution(2962667824422182617)
XLA Ops:
  11.5 4.6 fusion.92
  32.7 16.0 %while.26 = (s32[]{:T(128)}, bf16[2,512,8,64]{1,3,2,0:T(8,128)(2,1)}, f32[2,8,512]{2,1,0:T(8,128)S(1)}, bf16[2,512,8,64]{1,3,2,0:T(8,128)(2,1)}, s32[2,512]{1,0:...) while((s32[]{:T(128)}, bf16[2,512,8,64]{1,3,2,0:T(8,128)(2,1)}, ...), condition=%wide.region_3.4_spmd, body=%wide.region_0.3_spmd.sunk | while | flops 562556928 | bytes 32645240 | solution.py:198
  37.5 3.2 fusion.312
  45.4 3.2 fusion.312
  51.0 4.6 fusion.81
  61.1 26.0 %all-reduce.19.cloned.1.call-done = (f32[2,512,1024]{2,1,0:T(8,128)}, f32[2,512,16]{1,2,0:T(8,128)}) async-done(((f32[2,512,1024]{2,1,0:T(8,128)}, f32[2,512,16]{1,2,0:T(8,128)}), (f32[2,512,1024]{2,1,0:T(8,128)}, f32[2,512,16]{1,2,0:T(8,128)})) %all-reduce.19.cloned.1.call-update) | async-done | bytes 4259856 | tf_op jit(solution)/shard_map/psum | solution.py:200
  87.1 4.5 fusion.217
  95.3 4.5 fusion.74
  100.5 5.3 fusion.78
  105.8 20.0 %multiply_convert_fusion.1 = (bf16[2,512,2048]{2,1,0:T(8,128)(2,1)S(1)}, f32[2,512,2048]{2,1,0:T(8,128)}) fusion(f32[2,512,2048]{2,1,0:T(8,128)S(1)} %get-tuple-element.199, u8[512,2048]{1,0:T(8,128)(4,1)S(1)} %get-tuple-element.126, u8[512,2048]{1,0:T(8,128)(4,1)S(1)} %get-tuple-element.125), kind=kLoop, calls=%fused_computation.74 | loop fusion | flops 146800640 | bytes 23068672 | tf_op jit(solution)/shard_map/convert_element_type | solution.py:212
  125.8 6.1 %fusion.70 = f32[2,512,1024]{2,1,0:T(8,128)} fusion(bf16[2,512,2048]{2,1,0:T(8,128)(2,1)S(1)} %get-tuple-element.187, bf16[2048,1024]{1,0:T(8,128)(2,1)S(1)} %copy-done.90), kind=kOutput, calls=%fused_computation.96 | convolution fusion | flops 4294967296 | bytes 12582912 | tf_op jit(solution)/shard_map/bhp,pz->bhz/dot_general | solution.py:42
  134.1 29.6 %all-reduce.17.cloned.1.call-done = (f32[2,512,1024]{2,1,0:T(8,128)}, f32[2,512,16]{1,2,0:T(8,128)}) async-done(((f32[2,512,1024]{2,1,0:T(8,128)}, f32[2,512,16]{1,2,0:T(8,128)}), (f32[2,512,1024]{2,1,0:T(8,128)}, f32[2,512,16]{1,2,0:T(8,128)})) %all-reduce.17.cloned.1.call-update) | async-done | bytes 4259856 | tf_op jit(solution)/shard_map/psum | solution.py:213
  163.8 6.4 %fusion.218 = (f32[2,512]{1,0:T(2,128)S(1)}, f32[2,512,1024]{2,1,0:T(8,128)S(1)}) fusion(f32[2,512,1024]{2,1,0:T(8,128)} %get-tuple-element.181, f32[2,512,16]{1,2,0:T(8,128)} %get-tuple-element.182, bf16[2,16,1024]{2,0,1:T(2,128)(2,1)S(1)} %convolution_convert_fusion.2, f32[1024]{0:T(1024)S(1)} %copy-done.87, f32[1024]{0:T(1024)S(1)} %copy-done.83, ...), kind=kOutput, calls=%fused_computation.286 | convolution fusion | flops 208665600 | bytes 12734464 | tf_op jit(solution)/shard_map/slr,srn->sln/dot_general | solution.py:26
  171.4 3.7 add_add_fusion.1
  181.6 7.0 %fusion.68 = f32[2,512,2048]{2,1,0:T(8,128)} fusion(bf16[2,512,1024]{2,1,0:T(8,128)(2,1)S(1)} %add_convert_fusion.4, bf16[2048,1024]{1,0:T(8,128)(2,1)S(1)} %copy-done.91), kind=kOutput, calls=%fused_computation.94 | convolution fusion | flops 4294967296 | bytes 14680064 | tf_op jit(solution)/shard_map/zpi,hi->zph/dot_general | solution.py:48
  188.5 8.2 %add_convert_fusion = bf16[2,512,2048]{2,1,0:T(8,128)(2,1)S(1)} fusion(f32[2,512,2048]{2,1,0:T(8,128)} %get-tuple-element.188, f32[2,512,2048]{2,1,0:T(8,128)} %fusion.68, f32[2,512,2048]{2,1,0:T(8,128)S(1)} %bitcast.297, bf16[2,512,16]{1,2,0:T(8,128)(2,1)S(1)} %convolution_convert_fusion.9, bf16[2,2048,16]{1,0,2:T(2,128)(2,1)S(1)} %copy-done.49), kind=kOutput, calls=%fused_computation.73 | convolution fusion | flops 98566144 | bytes 29523968 | tf_op jit(solution)/shard_map/kyg,kxg->kyx/dot_general | solution.py:60
  196.8 6.1 %fusion.72 = f32[2,512,1024]{2,1,0:T(8,128)} fusion(bf16[2,512,2048]{2,1,0:T(8,128)(2,1)S(1)} %add_convert_fusion, bf16[1024,2048]{1,0:T(8,128)(2,1)S(1)} %copy-done.93), kind=kOutput, calls=%fused_computation.98 | convolution fusion | flops 4294967296 | bytes 12582912 | tf_op jit(solution)/shard_map/zpi,hi->zph/dot_general | solution.py:48
  206.6 28.2 %all-reduce.15.cloned.1.call-done = (f32[2,512,1024]{2,1,0:T(8,128)}, f32[2,512,16]{1,2,0:T(8,128)}) async-done(((f32[2,512,1024]{2,1,0:T(8,128)}, f32[2,512,16]{1,2,0:T(8,128)}), (f32[2,512,1024]{2,1,0:T(8,128)}, f32[2,512,16]{1,2,0:T(8,128)})) %all-reduce.15.cloned.1.call-update) | async-done | bytes 4259856 | tf_op jit(solution)/shard_map/psum | solution.py:233
  234.8 7.6 %multiply_reduce_fusion.1 = (f32[2,512]{1,0:T(2,128)S(1)}, f32[2,512,1024]{2,1,0:T(8,128)S(1)}) fusion(f32[2,512,1024]{2,1,0:T(8,128)} %copy-done.2, f32[2,512]{1,0:T(2,128)S(1)} %broadcast_multiply_fusion.1, f32[1024]{0:T(1024)S(1)} %copy-done.83, f32[2,512,16]{1,2,0:T(8,128)} %get-tuple-element.180, ...), kind=kOutput, calls=%fused_computation.104 | convolution fusion | flops 208665600 | bytes 16924672 | tf_op jit(solution)/shard_map/kyg,kxg->kyx/dot_general | solution.py:26
  250.5 25.7 %while.27 = (s32[]{:T(128)}, bf16[2,512,8,64]{1,3,2,0:T(8,128)(2,1)}, bf16[2,512,8,64]{1,3,2,0:T(8,128)(2,1)}, bf16[2,512,8,64]{1,3,2,0:T(8,128)(2,1)S(1)}, bf16...) while((s32[]{:T(128)}, ...), condition=%wide.region_20.21_spmd, body=%wide.region_18.20_spmd.sunk | while | flops 1375203328 | bytes 94498088 | solution.py:252
  283.3 3.3 add_add_fusion.2
  307.9 9.0 %all-reduce.13.cloned.1.call-done = (f32[2,512,16]{1,2,0:T(8,128)}, f32[2,512,16]{1,2,0:T(8,128)}, f32[2,512,1024]{2,1,0:T(8,128)}, f32[2,512,16]{1,2,0:T(8,128)}) async-done(((f32[2,512,16]{1,2,0:T(8,128)}, f32[2,512,16]{1,2,0:T(8,128)}, f32[2,512,1024]{2,1,0:T(8,128)}, f32[2,512,16]{1,2,0:T(8,128)}), (f32[2,512,16]{1,2,0:T(8,128)}, f32[2,512,16]{1,2,0:T(8,128)}, f32[2,512,1024]{2,1,0:T(8,128)}, ...) | async-done | bytes 4390928 | tf_op jit(solution)/shard_map/psum | solution.py:275
  329.4 4.3 add_convert_fusion.1
  333.7 215.4 %all-reduce.11.cloned.1.call-done = (f32[8,1024,16]{1,0,2:T(8,128)}, f32[8,16,512]{2,0,1:T(8,128)}, f32[8,1024,16]{1,0,2:T(8,128)}, f32[8,16,512]{2,0,1:T(8,128)...) async-done(((f32[8,1024,16]{1,0,2:T(8,128)}, ...) | async-done | bytes 6291472 | tf_op jit(solution)/shard_map/psum | solution.py:305
  (343 shorter events, 145.4 us)
Async XLA Ops:
  7.2 43.8 %copy-start = (bf16[512,1024]{1,0:T(8,128)(2,1)S(1)}, bf16[512,1024]{1,0:T(8,128)(2,1)}, u32[]{:S(2)}) copy-start(bf16[512,1024]{1,0:T(8,128)(2,1)} %param.37) | copy-start | bytes 3145732
  7.2 79.9 %all-reduce.19.cloned.1.call-start = ((), (), s32[]{:S(2)}) async-start(), calls=%async_computation.4 | async-start | bytes 8519680 | tf_op jit(solution)/shard_map/psum | solution.py:200
  11.5 13.8 %copy-start.54 = (bf16[2,16,512]{2,1,0:T(8,128)(2,1)}, bf16[2,16,512]{2,1,0:T(8,128)(2,1)S(1)}, u32[]{:S(2)}) copy-start(bf16[2,16,512]{2,1,0:T(8,128)(2,1)S(1)} %convolution_convert_fusion.17) | copy-start | bytes 98308
  16.4 9.0 %copy-start.74 = (bf16[2,16,512]{2,0,1:T(2,128)(2,1)}, bf16[2,16,512]{2,0,1:T(2,128)(2,1)S(1)}, u32[]{:S(2)}) copy-start(bf16[2,16,512]{2,0,1:T(2,128)(2,1)S(1)} %convolution_convert_fusion.16) | copy-start | bytes 98308
  18.0 10.6 %copy-start.52 = (bf16[2,16,512]{2,1,0:T(8,128)(2,1)}, bf16[2,16,512]{2,1,0:T(8,128)(2,1)S(1)}, u32[]{:S(2)}) copy-start(bf16[2,16,512]{2,1,0:T(8,128)(2,1)S(1)} %convolution_convert_fusion.15) | copy-start | bytes 98308
  32.7 16.0 %copy-start.97 = (bf16[8,512,16]{1,2,0:T(8,128)(2,1)S(1)}, bf16[8,512,16]{1,2,0:T(8,128)(2,1)}, u32[]{:S(2)}) copy-start(bf16[8,512,16]{1,2,0:T(8,128)(2,1)} %param.50) | copy-start | bytes 393220
  55.6 108.1 %all-reduce.17.cloned.1.call-start = ((), (), s32[]{:S(2)}) async-start(), calls=%async_computation.3 | async-start | bytes 8519680 | tf_op jit(solution)/shard_map/psum | solution.py:213
  105.8 20.0 %copy-start.28 = (f32[2,512,2048]{2,1,0:T(8,128)}, f32[2,512,2048]{2,1,0:T(8,128)S(1)}, u32[]{:S(2)}) copy-start(f32[2,512,2048]{2,1,0:T(8,128)S(1)} %get-tuple-element.199) | copy-start | bytes 25165828
  105.8 20.0 %copy-start.90 = (bf16[2048,1024]{1,0:T(8,128)(2,1)S(1)}, bf16[2048,1024]{1,0:T(8,128)(2,1)}, u32[]{:S(2)}) copy-start(bf16[2048,1024]{1,0:T(8,128)(2,1)} %param.39) | copy-start | bytes 12582916
  133.8 101.0 %all-reduce.15.cloned.1.call-start = ((), (), s32[]{:S(2)}) async-start(), calls=%async_computation.2 | async-start | bytes 8519680 | tf_op jit(solution)/shard_map/psum | solution.py:233
  204.8 112.0 %all-reduce.13.cloned.1.call-start = ((), (), s32[]{:S(2)}) async-start(), calls=%async_computation.1 | async-start | bytes 8781824 | tf_op jit(solution)/shard_map/psum | solution.py:275
  286.6 262.4 %all-reduce.11.cloned.1.call-start = ((), (), s32[]{:S(2)}) async-start(), calls=%async_computation | async-start | bytes 12582912 | tf_op jit(solution)/shard_map/psum | solution.py:305
  293.3 8.6 %copy-start.53 = (bf16[2,16,512]{2,1,0:T(8,128)(2,1)S(1)}, bf16[2,16,512]{2,1,0:T(8,128)(2,1)}, u32[]{:S(2)}) copy-start(bf16[2,16,512]{2,1,0:T(8,128)(2,1)} %copy-done.52) | copy-start | bytes 98308
  294.0 9.4 %copy-start.14 = (bf16[2,512,1024]{2,1,0:T(8,128)(2,1)S(1)}, bf16[2,512,1024]{2,1,0:T(8,128)(2,1)}, u32[]{:S(2)}) copy-start(bf16[2,512,1024]{2,1,0:T(8,128)(2,1)} %copy-done.13) | copy-start | bytes 6291460
  294.0 9.4 %copy-start.58 = (f32[2,512,16]{1,2,0:T(8,128)S(1)}, f32[2,512,16]{1,2,0:T(8,128)}, u32[]{:S(2)}) copy-start(f32[2,512,16]{1,2,0:T(8,128)} %get-tuple-element.184) | copy-start | bytes 196612
  295.8 9.8 %copy-start.12 = (bf16[2,512,1024]{2,1,0:T(8,128)(2,1)S(1)}, bf16[2,512,1024]{2,1,0:T(8,128)(2,1)}, u32[]{:S(2)}) copy-start(bf16[2,512,1024]{2,1,0:T(8,128)(2,1)} %copy-done.11) | copy-start | bytes 6291460
  295.8 9.8 %copy-start.59 = (f32[2,512,16]{1,2,0:T(8,128)S(1)}, f32[2,512,16]{1,2,0:T(8,128)}, u32[]{:S(2)}) copy-start(f32[2,512,16]{1,2,0:T(8,128)} %get-tuple-element.180) | copy-start | bytes 196612
  300.4 16.4 %copy-start.5 = (bf16[1024,1024]{1,0:T(8,128)(2,1)S(1)}, bf16[1024,1024]{1,0:T(8,128)(2,1)}, u32[]{:S(2)}) copy-start(bf16[1024,1024]{1,0:T(8,128)(2,1)} %param.30) | copy-start | bytes 6291460
  549.0 9.2 %copy-start.44 = (f32[8,1024,16]{1,0,2:T(8,128)S(1)}, f32[8,1024,16]{1,0,2:T(8,128)}, u32[]{:S(2)}) copy-start(f32[8,1024,16]{1,0,2:T(8,128)} %get-tuple-element.167) | copy-start | bytes 1572868
  549.0 10.3 %copy-start.43 = (f32[8,16,1024]{2,0,1:T(8,128)S(1)}, f32[8,16,1024]{2,0,1:T(8,128)}, u32[]{:S(2)}) copy-start(f32[8,16,1024]{2,0,1:T(8,128)} %get-tuple-element.170) | copy-start | bytes 1572868
  552.0 9.5 %copy-start.71 = (f32[8,16,512]{2,0,1:T(8,128)S(1)}, f32[8,16,512]{2,0,1:T(8,128)}, u32[]{:S(2)}) copy-start(f32[8,16,512]{2,0,1:T(8,128)} %get-tuple-element.164) | copy-start | bytes 786436
  552.0 10.4 %copy-start.70 = (f32[8,16,512]{2,0,1:T(8,128)S(1)}, f32[8,16,512]{2,0,1:T(8,128)}, u32[]{:S(2)}) copy-start(f32[8,16,512]{2,0,1:T(8,128)} %get-tuple-element.166) | copy-start | bytes 786436
  554.9 9.2 %copy-start.68 = (f32[8,512,16]{1,0,2:T(8,128)S(1)}, f32[8,512,16]{1,0,2:T(8,128)}, u32[]{:S(2)}) copy-start(f32[8,512,16]{1,0,2:T(8,128)} %get-tuple-element.169) | copy-start | bytes 786436
  554.9 10.1 %copy-start.1 = (bf16[512,1024]{1,0:T(8,128)(2,1)S(1)}, bf16[512,1024]{1,0:T(8,128)(2,1)}, u32[]{:S(2)}) copy-start(bf16[512,1024]{1,0:T(8,128)(2,1)} %param.37) | copy-start | bytes 3145732
  (88 other events, 367.1 us)
Sparse Core Ops, SparseCore 0:
  55.7 31.3 all-reduce.18
  133.9 29.8 all-reduce.16
  204.9 29.7 all-reduce.14
  286.7 30.1 all-reduce.12
  325.4 223.5 all-reduce.10
where the time goes:
time: 578 us; the launch traced here: 572 us
  waiting for transfers between devices  308 us (53%)
  matrix products  176 us (30%)
  other arithmetic  42.8 us (7%)
  local copies, waits for them, and re-layouts  28.4 us (5%)
  between operations  14.9 us (3%)
    psum x1, waiting for transfers between devices, on_device(): lax.psum((attention_parts[0], attention_parts[1], attention_parts[2], att...  215 us
    dot_general x12, matrix products, mixed(): jnp.einsum(form, left.astype(jnp.float32), right.astype(jnp.float32), pre...  34 us
    psum x1, waiting for transfers between devices, on_device(): lax.psum((project(hidden, contract_weight), low_rank(hidden, contract_low...  29.6 us
    psum x1, waiting for transfers between devices, on_device(): lax.psum((project_back(back_before, expand_weight), rank_back(back_before...  28.2 us
    psum x1, waiting for transfers between devices, on_device(): lax.psum((project(head_flat, output_weight), low_rank(head_flat, output_l...  26 us
    dot_general x6, matrix products, project(): jnp.einsum('bhp,pz->bhz', input_activation, dense_weight, preferred_eleme...  25 us
    unnamed x198, local copies, waits for them, and re-layouts  23 us
    dot_general x6, matrix products, project_back(): jnp.einsum('zpi,hi->zph', gradient_token_rows, dense_weight, preferred_el...  21.9 us
  transfers between devices with their start and end apart: 5, of which 5 were waited for; matrix products, arithmetic and copies ran while one was open for 6% of the time, Pallas kernels for 0%

commit v1 on v0

v1 whole, which is shorter than its diff:
```python
import jax
import jax.numpy as jnp
from jax import lax
from jax.experimental import pallas as pl
from jax.experimental.pallas import tpu as pltpu
from jax.sharding import PartitionSpec as P

HEAD_WIDTH = 64
RANK = 16
MESH = pl.DeviceIdType.MESH
F32 = jnp.float32
BF16 = jnp.bfloat16
EPS = 1e-05
ROWS = 64


def nn(a, b):
    return jnp.dot(a, b, preferred_element_type=F32)


def nt(a, b):
    return lax.dot_general(a, b, (((1,), (1,)), ((), ())), preferred_element_type=F32)


def split(v):
    hi = v.astype(BF16)
    return hi, (v - hi.astype(F32)).astype(BF16)


def nn_wide(v, b):
    hi, lo = split(v)
    return nn(hi, b) + nn(lo, b)


def gelu_parts(v):
    z = jnp.abs(v) * 0.7071067811865476
    t = 1.0 / (1.0 + 0.3275911 * z)
    e = jnp.exp(v * v * -0.5)
    tail = t * (
        0.127414796 + t * (-0.142248368 + t * (0.7107068705 + t * (-0.7265760135 + t * 0.5307027145)))
    ) * e
    cdf = jnp.where(v >= 0, 1.0 - tail, tail)
    return v * cdf, cdf + v * (e * 0.3989422804014327)


def layer_kernel(
    ids, seg, x_hbm, cot_hbm, wq, wk, wv, wo_hbm, we_hbm, wc_hbm, g1, b1, g2, b2,
    qd, kd, vd, qu, ku, vu, od, ou, ed, eu, cd, cu,
    out_hbm, grad_hbm, t_u, t_d, t_od, t_ou, t_eu, t_cd, t_ed, t_cu,
    x, cot, wp, wo, we, wc, dtab, utab, qkv, heads, bias, lse, xhat, rstd, hidden, slope, acc, recv,
    row, work, lcol, rank_t, rank_o, rank_e, rank_c, stage_out,
    load_sem, send_sem, recv_sem, out_sem, credit,
):
    dp = lax.axis_index("dp")
    core = lax.axis_index("tensor")
    partner = (dp, 1 - core)
    first = (core == 0).astype(F32)

    def load(i, src, dst):
        cp = pltpu.make_async_copy(src, dst, load_sem.at[i])
        cp.start()
        return cp

    loads = [load(0, x_hbm, x)]
    tabs = []
    for i, (w, d, u) in enumerate(((wq, qd, qu), (wk, kd, ku), (wv, vd, vu))):
        tabs.append(load(1 + i, w, wp.at[i]))
        tabs.append(load(4 + i, d, dtab.at[i]))
        tabs.append(load(7 + i, u, utab.at[i]))
    load_wo = load(10, wo_hbm, wo)
    load_we = load(11, we_hbm, we)
    load_wc = load(12, wc_hbm, wc)
    load_cot = load(13, cot_hbm, cot)

    barrier = pltpu.get_barrier_semaphore()
    pl.semaphore_signal(barrier, inc=1, device_id=partner, device_id_type=MESH)
    pl.semaphore_wait(barrier, 1)

    def exchange(s):
        return pltpu.make_async_remote_copy(
            src_ref=acc.at[s], dst_ref=recv.at[s], send_sem=send_sem.at[s], recv_sem=recv_sem.at[s],
            device_id=partner, device_id_type=MESH,
        )

    def taken(s):
        pl.semaphore_signal(credit.at[s], inc=1, device_id=partner, device_id_type=MESH)

    def send(s):
        pl.semaphore_wait(credit.at[s], 1)
        exchange(s).start()

    n = x.shape[1]
    heads_half = heads.shape[2]
    pairs = heads_half // 128
    chunks = hidden.shape[2] // 512
    lane = lax.broadcasted_iota(jnp.int32, (n, 128), 1)
    low_half = lane < HEAD_WIDTH

    for cp in loads + tabs:
        cp.wait()

    def stage1(s, carry):
        aid = ids[s]
        xs = x.at[s]
        seg_row = seg[pl.ds(s, 1), :]
        seg_col = jnp.broadcast_to(seg_row, (128, n)).T
        for j in range(n // 128):
            same = seg_col == seg_row[:, j * 128:(j + 1) * 128]
            bias[s, :, j * 128:(j + 1) * 128] = jnp.where(same, 0.0, -1e30)

        def project(p, c):
            d_sel = dtab[p, aid]
            rank = nt(xs[...], d_sel).astype(BF16)
            rank_t[s, p] = nt(d_sel, xs[...]).astype(BF16)
            scale = jnp.where(p == 0, 0.125, 1.0)
            qkv[s, p] = ((nn(xs[...], wp[p]) + nn(rank, utab[p, aid])) * scale).astype(BF16)
            return c

        lax.fori_loop(0, 3, project, 0)

        def pair(hp, c):
            at = pl.ds(pl.multiple_of(hp * 128, 128), 128)
            k2 = qkv[s, 1, :, at]
            v2 = jnp.concatenate([qkv[s, 2, :, at], jnp.ones((n, 128), BF16)], axis=1)
            for r in range(2):
                rows = slice(r * (n // 2), (r + 1) * (n // 2))
                q2 = qkv[s, 0, rows, at]
                outs = []
                ln = lane[rows]
                for j in range(2):
                    mine = (ln < HEAD_WIDTH) if j == 0 else (ln >= HEAD_WIDTH)
                    score = nt(jnp.where(mine, q2, jnp.zeros_like(q2)), k2) + bias[s, rows, :]
                    top = jnp.max(score, axis=1, keepdims=True)
                    e = jnp.exp(score - top).astype(BF16)
                    both = nn(e, v2)
                    total = both[:, 128:]
                    outs.append(both[:, :128] / total)
                    old = lcol[rows, :]
                    lcol[rows, :] = jnp.where(ln == 2 * hp + j, top + jnp.log(total), old)
                heads[s, rows, at] = jnp.where(ln < HEAD_WIDTH, outs[0], outs[1]).astype(BF16)
            return c

        lax.fori_loop(0, pairs, pair, 0)
        lse[s] = lcol[...].T[:lse.shape[1], :]
        return carry

    def stage1_out(s, carry):
        aid = ids[s]
        od_sel = od[aid]
        hs = heads[s]
        rank_o[s] = nt(od_sel, hs)
        acc[s] = nn(hs, wo[...]) + nn_wide(nt(hs, od_sel), ou[aid])
        exchange(s).start()
        return carry

    def both1(s, carry):
        stage1(s, carry)

        @pl.when(s == 0)
        def _():
            load_wo.wait()

        stage1_out(s, carry)
        return carry

    lax.fori_loop(0, 2, both1, 0)

    def stage2(s, carry):
        aid = ids[s]
        exchange(s).wait()

        def norm(i, c):
            rows = pl.ds(pl.multiple_of(i * ROWS, ROWS), ROWS)
            h = x[s, rows, :].astype(F32) + (acc[s, rows, :] + recv[s, rows, :])
            mean = jnp.mean(h, axis=1, keepdims=True)
            h = h - mean
            inv = lax.rsqrt(jnp.mean(h * h, axis=1, keepdims=True) + EPS)
            h = h * inv
            xhat[s, rows, :] = h
            rstd[s, rows, :] = jnp.broadcast_to(inv, (ROWS, 128))
            row[rows, :] = (h * g1[...] + b1[...]).astype(BF16)
            return c

        lax.fori_loop(0, n // ROWS, norm, 0)
        taken(s)
        ed_sel = ed[aid]
        inner = row[...]
        rank = nt(inner, ed_sel).astype(BF16)
        rank_e[s] = nt(ed_sel, inner).astype(BF16)

        def chunk(c, ranks):
            rc, rct = ranks
            at = pl.ds(pl.multiple_of(c * 512, 512), 512)
            before = nn(row[...], we[:, at]) + nn(rank, eu[aid, :, at])
            hid, sl = gelu_parts(before)
            hid = hid.astype(BF16)
            hidden[s, :, at] = hid
            slope[s, :, at] = sl.astype(BF16)
            cd_sel = cd[aid, :, at]
            part = nn(hid, wc[at, :])

            @pl.when(c == 0)
            def _():
                acc[s] = part

            @pl.when(c > 0)
            def _():
                acc[s] += part

            return rc + nt(hid, cd_sel), rct + nt(cd_sel, hid)

        rc, rct = lax.fori_loop(
            0, chunks, chunk, (jnp.zeros((n, RANK), F32), jnp.zeros((RANK, n), F32))
        )
        rank_c[s] = rct
        acc[s] += nn_wide(rc, cu[aid])
        send(s)
        return carry

    load_we.wait()
    load_wc.wait()
    lax.fori_loop(0, 2, stage2, 0)

    def put_out(s):
        return pltpu.make_async_copy(stage_out.at[s], out_hbm.at[s], out_sem.at[s])

    def put_grad(s):
        return pltpu.make_async_copy(stage_out.at[s], grad_hbm.at[s], out_sem.at[s])

    def stage3(s, carry):
        aid = ids[s]
        exchange(s).wait()

        def norm(i, c):
            rows = pl.ds(pl.multiple_of(i * ROWS, ROWS), ROWS)
            normed = xhat[s, rows, :] * g1[...] + b1[...]
            h = normed + (acc[s, rows, :] + recv[s, rows, :])
            mean = jnp.mean(h, axis=1, keepdims=True)
            h = h - mean
            inv = lax.rsqrt(jnp.mean(h * h, axis=1, keepdims=True) + EPS)
            h = h * inv
            stage_out[s, rows, :] = (h * g2[...] + b2[...]).astype(BF16)
            u = cot[s, rows, :].astype(F32) * g2[...]
            back = inv * (
                u - jnp.mean(u, axis=1, keepdims=True) - h * jnp.mean(u * h, axis=1, keepdims=True)
            )
            acc[s, rows, :] = back * first
            row[rows, :] = back.astype(BF16)
            return c

        lax.fori_loop(0, n // ROWS, norm, 0)
        taken(s)
        put_out(s).start()
        cu_sel = cu[aid]
        back_outer = row[...]
        brc = nt(back_outer, cu_sel).astype(BF16)
        brc_t = nt(cu_sel, back_outer).astype(BF16)
        t_cu[s] = nn_wide(rank_c[s], back_outer)
        re_t = rank_e[s]

        def chunk(c, ranks):
            br, brt = ranks
            at = pl.ds(pl.multiple_of(c * 512, 512), 512)
            t_cd[s, :, at] = nn(brc_t, hidden[s, :, at])
            bh = nt(row[...], wc[at, :]) + nn(brc, cd[aid, :, at])
            bb = (bh * slope[s, :, at].astype(F32)).astype(BF16)
            t_eu[s, :, at] = nn(re_t, bb)
            acc[s] += nt(bb, we[:, at])
            eu_sel = eu[aid, :, at]
            return br + nt(bb, eu_sel), brt + nt(eu_sel, bb)

        br, brt = lax.fori_loop(
            0, chunks, chunk, (jnp.zeros((n, RANK), F32), jnp.zeros((RANK, n), F32))
        )
        acc[s] += nn_wide(br, ed[aid])
        send(s)
        inner = (xhat[s] * g1[...] + b1[...]).astype(BF16)
        t_ed[s] = nn_wide(brt, inner)
        return carry

    load_cot.wait()
    lax.fori_loop(0, 2, stage3, 0)

    d_out, d_q, d_k, d_v, dq_t = 0, 1, 2, 3, 4

    def stage4(s, carry):
        aid = ids[s]
        exchange(s).wait()

        def norm(i, c):
            rows = pl.ds(pl.multiple_of(i * ROWS, ROWS), ROWS)
            u = (acc[s, rows, :] + recv[s, rows, :]) * g1[...]
            h = xhat[s, rows, :]
            back = rstd[s, rows, 0:1] * (
                u - jnp.mean(u, axis=1, keepdims=True) - h * jnp.mean(u * h, axis=1, keepdims=True)
            )
            acc[s, rows, :] = back * first
            row[rows, :] = back.astype(BF16)
            return c

        lax.fori_loop(0, n // ROWS, norm, 0)
        taken(s)
        ou_sel = ou[aid]
        od_sel = od[aid]
        back_branch = row[...]
        bro = nt(back_branch, ou_sel).astype(BF16)
        bro_t = nt(ou_sel, back_branch).astype(BF16)
        t_ou[s] = nn_wide(rank_o[s], back_branch)
        hs = heads[s]
        t_od[s] = nn(bro_t, hs)
        d_heads = (nt(back_branch, wo[...]) + nn(bro, od_sel)).astype(BF16)
        work[d_out] = d_heads
        pick = (
            lax.broadcasted_iota(jnp.int32, (RANK, heads_half), 1) // HEAD_WIDTH
            == lax.broadcasted_iota(jnp.int32, (RANK, heads_half), 0)
        ).astype(BF16)
        hi, lo = split(d_heads.astype(F32) * hs.astype(F32))
        lcol[0:RANK, 0:128] = jnp.zeros((RANK, 128), F32)
        dots = nt(pick, hi) + nt(pick, lo)
        drow = rank_o.at[s]
        drow[...] = dots

        def pair(hp, c):
            at = pl.ds(pl.multiple_of(hp * 128, 128), 128)
            q2 = qkv[s, 0, :, at]
            k2 = qkv[s, 1, :, at]
            v2 = qkv[s, 2, :, at]
            do2 = work[d_out, :, at]
            k2t = k2.T
            zero = jnp.zeros_like(k2)
            dk, dv = [], []
            for j in range(2):
                mine = low_half if j == 0 else jnp.logical_not(low_half)
                h = 2 * hp + j
                st = nt(jnp.where(mine, k2, zero), q2) + bias[s]
                pt = jnp.exp(st - lse[s, pl.ds(h, 1), :])
                dpt = nt(jnp.where(mine, v2, zero), do2)
                dst = (pt * (dpt - drow[pl.ds(h, 1), :])).astype(BF16)
                dv.append(nn(pt.astype(BF16), do2))
                dk.append(nn(dst, q2))
                dqt = nn(k2t[j * HEAD_WIDTH:(j + 1) * HEAD_WIDTH, :], dst) * 0.125
                work[dq_t, pl.ds(pl.multiple_of(h * HEAD_WIDTH, HEAD_WIDTH), HEAD_WIDTH), :] = dqt.astype(BF16)
            work[d_k, :, at] = jnp.where(low_half, dk[0], dk[1]).astype(BF16)
            work[d_v, :, at] = jnp.where(low_half, dv[0], dv[1]).astype(BF16)
            return c

        lax.fori_loop(0, pairs, pair, 0)
        work[d_q] = work[dq_t].T

        def project(p, c):
            dp_ = work[1 + p]
            u_sel = utab[p, aid]
            d_sel = dtab[p, aid]
            t_u[s, p] = nn(rank_t[s, p], dp_)
            t_d[s, p] = nn_wide(nt(u_sel, dp_), x[s])
            acc[s] += nt(dp_, wp[p]) + nn_wide(nt(dp_, u_sel), d_sel)
            return c

        lax.fori_loop(0, 3, project, 0)
        send(s)
        return carry

    lax.fori_loop(0, 2, stage4, 0)

    def stage5(s, carry):
        exchange(s).wait()
        put_out(s).wait()

        def add(i, c):
            rows = pl.ds(pl.multiple_of(i * ROWS, ROWS), ROWS)
            stage_out[s, rows, :] = (acc[s, rows, :] + recv[s, rows, :]).astype(BF16)
            return c

        lax.fori_loop(0, n // ROWS, add, 0)
        put_grad(s).start()
        return carry

    lax.fori_loop(0, 2, stage5, 0)
    put_grad(0).wait()
    put_grad(1).wait()


def layer(ids, seg, x, cot, wq, wk, wv, wo, we, wc, g1, b1, g2, b2, *tables):
    s, n, d = x.shape
    hw = wq.shape[1]
    f = we.shape[1]
    hbm = pl.BlockSpec(memory_space=pl.ANY)
    vm = pl.BlockSpec(memory_space=pltpu.VMEM)
    sm = pl.BlockSpec(memory_space=pltpu.SMEM)
    sds = jax.ShapeDtypeStruct
    return pl.pallas_call(
        layer_kernel,
        out_shape=(
            sds((s, n, d), BF16), sds((s, n, d), BF16),
            sds((s, 3, RANK, hw), F32), sds((s, 3, RANK, d), F32), sds((s, RANK, hw), F32),
            sds((s, RANK, d), F32), sds((s, RANK, f), F32), sds((s, RANK, f), F32),
            sds((s, RANK, d), F32), sds((s, RANK, d), F32),
        ),
        in_specs=[sm, vm, hbm, hbm, hbm, hbm, hbm, hbm, hbm, hbm, vm, vm, vm, vm]
        + [hbm] * 6 + [vm] * 6,
        out_specs=(hbm, hbm) + (vm,) * 8,
        scratch_shapes=[
            pltpu.VMEM((s, n, d), BF16),
            pltpu.VMEM((s, n, d), BF16),
            pltpu.VMEM((3, d, hw), BF16),
            pltpu.VMEM((hw, d), BF16),
            pltpu.VMEM((d, f), BF16),
            pltpu.VMEM((f, d), BF16),
            pltpu.VMEM((3, 8, RANK, d), BF16),
            pltpu.VMEM((3, 8, RANK, hw), BF16),
            pltpu.VMEM((s, 3, n, hw), BF16),
            pltpu.VMEM((s, n, hw), BF16),
            pltpu.VMEM((s, n, n), F32),
            pltpu.VMEM((s, RANK, n), F32),
            pltpu.VMEM((s, n, d), F32),
            pltpu.VMEM((s, n, 128), F32),
            pltpu.VMEM((s, n, f), BF16),
            pltpu.VMEM((s, n, f), BF16),
            pltpu.VMEM((s, n, d), F32),
            pltpu.VMEM((s, n, d), F32),
            pltpu.VMEM((n, d), BF16),
            pltpu.VMEM((5, n, hw), BF16),
            pltpu.VMEM((n, 128), F32),
            pltpu.VMEM((s, 3, RANK, n), BF16),
            pltpu.VMEM((s, RANK, n), F32),
            pltpu.VMEM((s, RANK, n), BF16),
            pltpu.VMEM((s, RANK, n), F32),
            pltpu.VMEM((s, n, d), BF16),
            pltpu.SemaphoreType.DMA((14,)),
            pltpu.SemaphoreType.DMA((2,)),
            pltpu.SemaphoreType.DMA((2,)),
            pltpu.SemaphoreType.DMA((2,)),
            pltpu.SemaphoreType.REGULAR((2,)),
        ],
        compiler_params=pltpu.CompilerParams(
            collective_id=0, has_side_effects=True, vmem_limit_bytes=63 * 1024 * 1024
        ),
    )(ids, seg, x, cot, wq, wk, wv, wo, we, wc, g1, b1, g2, b2, *tables)


def on_device(
    tokens, cotangent, segment_ids, adapter_ids, query_weight, key_weight, value_weight, output_weight,
    expand_weight, contract_weight, first_gain, first_shift, second_gain, second_shift,
    query_down, query_up, key_down, key_up, value_down, value_up, output_down, output_up,
    expand_down, expand_up, contract_down, contract_up,
):
    seqs, length = segment_ids.shape
    width = tokens.shape[1]
    turn = lambda t: jnp.swapaxes(t, 1, 2)
    line = lambda v: v.reshape(1, -1)
    out, grad, t_u, t_d, t_od, t_ou, t_eu, t_cd, t_ed, t_cu = layer(
        adapter_ids, segment_ids.astype(F32),
        tokens.reshape(seqs, length, width), cotangent.reshape(seqs, length, width),
        query_weight, key_weight, value_weight, output_weight, expand_weight, contract_weight,
        line(first_gain), line(first_shift), line(second_gain), line(second_shift),
        turn(query_down), turn(key_down), turn(value_down), query_up, key_up, value_up,
        turn(output_down), output_up, turn(expand_down), expand_up, turn(contract_down), contract_up,
    )
    selector = (
        adapter_ids[:, None] == jnp.arange(query_down.shape[0], dtype=jnp.int32)[None, :]
    ).astype(F32)
    spread = lambda t: jnp.einsum("se,s...->e...", selector, t, precision=lax.Precision.HIGHEST)
    both = lax.psum((spread(t_d), spread(t_ou), spread(t_ed), spread(t_cu)), ("dp", "tensor"))
    one = lax.psum((spread(t_u), spread(t_od), spread(t_eu), spread(t_cd)), "dp")
    g_d, g_ou, g_ed, g_cu = both
    g_u, g_od, g_eu, g_cd = one
    return (
        out.reshape(tokens.shape), grad.reshape(tokens.shape),
        turn(g_d[:, 0]), g_u[:, 0], turn(g_d[:, 1]), g_u[:, 1], turn(g_d[:, 2]), g_u[:, 2],
        turn(g_od), g_ou, turn(g_ed), g_eu, turn(g_cd), g_cu,
    )


def solution(mesh):
    cols = P(None, None, "tensor")
    mid = P(None, "tensor", None)
    return jax.shard_map(
        on_device,
        mesh=mesh,
        in_specs=(
            P("dp", None), P("dp", None), P("dp", None), P("dp"),
            P(None, "tensor"), P(None, "tensor"), P(None, "tensor"), P("tensor", None),
            P(None, "tensor"), P("tensor", None), P(), P(), P(), P(),
            P(), cols, P(), cols, P(), cols, mid, P(), P(), cols, mid, P(),
        ),
        out_specs=(
            P("dp", None), P("dp", None), P(), cols, P(), cols, P(), cols, mid, P(), P(), cols, mid, P(),
        ),
        check_vma=False,
    )
```

time: 578 us -> 448 us (0.78); the launches traced: 572 us -> 448 us
  matrix products: 176 us -> 15.3 us
  Pallas kernels: 0 us -> 115 us
  other arithmetic: 42.8 us -> 1.28 us
  waiting for transfers between devices: 308 us -> 282 us
  local copies, waits for them, and re-layouts: 28.4 us -> 19.6 us
    dot_general x86 -> x8, matrix products: 176 us -> 15.3 us  [on_device(): jnp.einsum('se,s...->e...', selector, t, precision=lax.Precision.HIGHEST)]
    pallas_call x0 -> x1, Pallas kernels: none -> 115 us  [layer(): pl.pallas_call(layer_kernel, out_shape=(sds((s, n, d), BF16), sds((s, n,...]
    convert_element_type x6 -> x1, other arithmetic: 29 us -> 1.28 us  [on_device(): segment_ids.astype(F32)]
    psum x5 -> x2, waiting for transfers between devices: 308 us -> 282 us  [the longest x1 147 us: on_device(): lax.psum((spread(t_u), spread(t_od), spread(t_eu), spread(t_cd)), 'dp')]
    reduce_sum x6 -> x0, other arithmetic: 9.16 us -> none  [the longest x2 4.05 us: layer_norm(): centered = summed - average]
    unnamed x198 -> x42, local copies, waits for them, and re-layouts: 23 us -> 16.9 us
  transfers between devices with their start and end apart: 5 -> 2, of which waited for: 5 -> 2; matrix products, arithmetic and copies ran while one was open for 6% -> 3% of each run, Pallas kernels for 0% -> 0%
where the time goes in v1:
time: 448 us
  waiting for transfers between devices  282 us (63%)
  Pallas kernels  115 us (26%)
  local copies, waits for them, and re-layouts  19.6 us (4%)
  matrix products  15.3 us (3%)
  between operations  14.1 us (3%)
    psum x1, waiting for transfers between devices, on_device(): lax.psum((spread(t_u), spread(t_od), spread(t_eu), spread(t_cd)), 'dp')  147 us
    psum x1, waiting for transfers between devices, on_device(): lax.psum((spread(t_d), spread(t_ou), spread(t_ed), spread(t_cu)), ('dp',...  135 us
    pallas_call x1, Pallas kernels, layer(): pl.pallas_call(layer_kernel, out_shape=(sds((s, n, d), BF16), sds((s, n,...  115 us
    unnamed x42, local copies, waits for them, and re-layouts  16.9 us
    dot_general x8, matrix products, on_device(): jnp.einsum('se,s...->e...', selector, t, precision=lax.Precision.HIGHEST)  15.3 us
  transfers between devices with their start and end apart: 2, of which 2 were waited for; matrix products, arithmetic and copies ran while one was open for 3% of the time, Pallas kernels for 0%

profile of v1, /device:TPU:0, one launch (start us, length us, event | category | flops | bytes accessed | tf_op | source)
XLA Modules:
  0.0 447.9 jit_solution(17545302762565384699)
XLA Ops:
  7.2 1.3 convert_element_type.4.seg
  8.5 115.4 %shard_map.353 = (bf16[2,512,1024]{2,1,0:T(8,128)(2,1)}, bf16[2,512,1024]{2,1,0:T(8,128)(2,1)}, f32[2,3,16,512]{3,2,1,0:T(8,128)}, f32[2,3,16,1024]{3,2,1,0:T(8,...) custom-call(s32[2]{0:T(128)} %ids.1, ...), custom_call_target="tpu_custom_call" | custom-call | tf_op jit(solution)/shard_map/pallas_call | solution.py:391
  123.9 2.3 fusion.10
  126.2 2.2 convolution_bitcast_fusion.1
  128.4 2.2 fusion.7
  130.6 2.3 fusion
  133.3 1.1 convolution_bitcast_fusion.2
  134.4 1.6 fusion.5
  135.9 1.8 fusion.3
  137.8 1.8 convolution_bitcast_fusion
  139.6 134.6 %all-reduce.5.cloned.1.call-done = (f32[8,3,16,1024]{3,0,2,1:T(8,128)}, f32[8,16,1024]{2,0,1:T(8,128)}, f32[8,1024,16]{1,0,2:T(8,128)}, f32[8,16,1024]{2,0,1:T(8,128)}) async-done(((f32[8,3,16,1024]{3,0,2,1:T(8,128)}, f32[8,16,1024]{2,0,1:T(8,128)}, f32[8,1024,16]{1,0,2:T(8,128)}, f32[8,16,1024]{2,0,1:T(8,128)}), (f32[8,3,16,1024]{3,0,2,1:T(8,128)}, f32[8,16,1024]{2,0,1:T(8,128)}, f32[8,1024,16]{1,0,2:T(8,128)}, ...) | async-done | bytes 3145744 | tf_op jit(solution)/shard_map/psum | solution.py:463
  274.3 1.5 slice_bitcast_fusion
  275.7 1.1 copy.52
  276.8 1.1 copy.50
  277.9 1.1 copy.48
  279.0 1.1 copy.55
  280.2 1.1 copy.56
  281.3 1.1 copy.59
  282.4 147.2 %all-reduce.7.cloned.1.call-done = (f32[8,3,16,512]{3,0,2,1:T(8,128)}, f32[8,512,16]{1,0,2:T(8,128)}, f32[8,16,2048]{2,0,1:T(8,128)}, f32[8,2048,16]{1,0,2:T(8,128)}) async-done(((f32[8,3,16,512]{3,0,2,1:T(8,128)}, f32[8,512,16]{1,0,2:T(8,128)}, f32[8,16,2048]{2,0,1:T(8,128)}, f32[8,2048,16]{1,0,2:T(8,128)}), (f32[8,3,16,512]{3,0,2,1:T(8,128)}, f32[8,512,16]{1,0,2:T(8,128)}, f32[8,16,2048]{2,0,1:T(8,128)}, ...) | async-done | bytes 3145744 | tf_op jit(solution)/shard_map/psum | solution.py:464
  429.5 1.3 slice_bitcast_fusion.3
  434.3 1.6 copy.57
  435.8 1.6 copy.58
  437.4 1.3 copy.87
  439.8 1.3 copy.88
  (36 shorter events, 4.8 us)
Async XLA Ops:
  7.2 267.1 %all-reduce.5.cloned.1.call-start = ((), (), s32[]{:S(2)}) async-start(), calls=%async_computation | async-start | bytes 6291456 | tf_op jit(solution)/shard_map/psum | solution.py:463
  8.5 115.4 %copy-start.13 = (s32[2]{0:T(128)S(1)}, s32[2]{0:T(128)}, u32[]{:S(2)}) copy-start(s32[2]{0:T(128)} %ids.1) | copy-start | bytes 28
  123.9 6.7 %copy-start.7 = (f32[2,3,16,1024]{3,2,1,0:T(8,128)S(1)}, f32[2,3,16,1024]{3,2,1,0:T(8,128)}, u32[]{:S(2)}) copy-start(f32[2,3,16,1024]{3,2,1,0:T(8,128)} %get-tuple-element.26) | copy-start | bytes 1179652
  130.6 2.7 copy-start.12
  133.0 1.4 copy-start.11
  133.0 3.0 copy-start.9
  133.0 4.8 %copy-start.8 = (f32[2,16,2048]{2,1,0:T(8,128)S(1)}, f32[2,16,2048]{2,1,0:T(8,128)}, u32[]{:S(2)}) copy-start(f32[2,16,2048]{2,1,0:T(8,128)} %get-tuple-element.32) | copy-start | bytes 786436
  133.0 296.5 %all-reduce.7.cloned.1.call-start = ((), (), s32[]{:S(2)}) async-start(), calls=%async_computation.1 | async-start | bytes 6291456 | tf_op jit(solution)/shard_map/psum | solution.py:464
  275.7 3.3 copy-start.6
  275.7 4.4 copy-start.5
  276.8 4.4 copy-start.4
  429.5 3.9 copy-start.10
  429.5 4.7 %copy-start.3 = (f32[8,16,2048]{2,0,1:T(8,128)S(1)}, f32[8,16,2048]{2,0,1:T(8,128)}, u32[]{:S(2)}) copy-start(f32[8,16,2048]{2,0,1:T(8,128)} %get-tuple-element.54) | copy-start | bytes 3145732
  430.8 5.0 %copy-start.2 = (f32[8,2048,16]{1,0,2:T(8,128)S(1)}, f32[8,2048,16]{1,0,2:T(8,128)}, u32[]{:S(2)}) copy-start(f32[8,2048,16]{1,0,2:T(8,128)} %get-tuple-element.55) | copy-start | bytes 3145732
  434.2 3.2 copy-start.1
  437.4 2.3 copy-start
Sparse Core Ops, SparseCore 0:
  133.1 141.0 all-reduce.4
  282.4 147.0 all-reduce.6

commit v2 on v1

--- a/solution.py
+++ b/solution.py
@@ -12,6 +12,8 @@
 BF16 = jnp.bfloat16
 EPS = 1e-05
 ROWS = 64
+GROUP = 16
+EARLY, LATE = 640, 512
 
 
 def nn(a, b):
@@ -46,15 +48,20 @@
 def layer_kernel(
     ids, seg, x_hbm, cot_hbm, wq, wk, wv, wo_hbm, we_hbm, wc_hbm, g1, b1, g2, b2,
     qd, kd, vd, qu, ku, vu, od, ou, ed, eu, cd, cu,
-    out_hbm, grad_hbm, t_u, t_d, t_od, t_ou, t_eu, t_cd, t_ed, t_cu,
+    out_hbm, grad_hbm, geu, ger, glu, glr, her, hlr,
     x, cot, wp, wo, we, wc, dtab, utab, qkv, heads, bias, lse, xhat, rstd, hidden, slope, acc, recv,
-    row, work, lcol, rank_t, rank_o, rank_e, rank_c, stage_out,
-    load_sem, send_sem, recv_sem, out_sem, credit,
+    row, work, lcol, rank_t, rank_e, drow, mine_rk, their_rk, stage_out,
+    pick_mine, picks, pack_e, pack_l, rs_e, rs_l, dense_eu, dense_er, dense_lu, dense_lr,
+    load_sem, send_sem, recv_sem, out_sem, credit, rk_send, rk_recv, pick_send, pick_recv,
+    rs_send_sem, rs_recv_sem, z_send, z_recv, plane_send, plane_recv, own_sem, swap_send, swap_recv,
 ):
     dp = lax.axis_index("dp")
     core = lax.axis_index("tensor")
     partner = (dp, 1 - core)
     first = (core == 0).astype(F32)
+    me = lax.rem(dp, GROUP)
+    base = dp - me
+    half = pl.ds(pl.multiple_of(core * 512, 512), 512)
 
     def load(i, src, dst):
         cp = pltpu.make_async_copy(src, dst, load_sem.at[i])
@@ -72,9 +79,158 @@
     load_wc = load(12, wc_hbm, wc)
     load_cot = load(13, cot_hbm, cot)
 
+    def peer(k):
+        return (base + lax.bitwise_xor(me, k), core)
+
     barrier = pltpu.get_barrier_semaphore()
     pl.semaphore_signal(barrier, inc=1, device_id=partner, device_id_type=MESH)
-    pl.semaphore_wait(barrier, 1)
+
+    def greet(k, c):
+        pl.semaphore_signal(barrier, inc=1, device_id=peer(k), device_id_type=MESH)
+        return c
+
+    lax.fori_loop(1, GROUP, greet, 0)
+    pl.semaphore_wait(barrier, GROUP)
+
+    def remote(src, dst, ss, rs, to):
+        return pltpu.make_async_remote_copy(
+            src_ref=src, dst_ref=dst, send_sem=ss, recv_sem=rs, device_id=to, device_id_type=MESH
+        )
+
+    def pick_copy(k):
+        return remote(pick_mine, picks.at[me], pick_send.at[k], pick_recv.at[k], peer(k))
+
+    table_id = lax.broadcasted_iota(jnp.int32, (8, 128), 0)
+    for s in range(2):
+        pick_mine[s] = (table_id == ids[s]).astype(F32)
+    picks[me] = pick_mine[...]
+
+    def send_pick(k, c):
+        pick_copy(k).start()
+        return c
+
+    lax.fori_loop(1, GROUP, send_pick, 0)
+
+    def rk_copy(s, i):
+        rows = pl.ds(i * RANK, RANK if i < 3 else 3 * RANK)
+        return remote(
+            mine_rk.at[s, rows], their_rk.at[s, rows], rk_send.at[s, i], rk_recv.at[s, i], partner
+        )
+
+    def rank_sum(s, i, rows):
+        rk_copy(s, i).wait()
+        at = slice(i * RANK, i * RANK + rows)
+        return mine_rk[s, at, :] + their_rk[s, at, :]
+
+    packs, parts, swapped = (pack_e, pack_l), (rs_e, rs_l), (her, hlr)
+    denses, gathered = ((dense_eu, dense_er), (dense_lu, dense_lr)), ((geu, ger), (glu, glr))
+
+    def shard_copy(g, s, k):
+        to = lax.bitwise_xor(me, k)
+        return remote(
+            packs[g].at[s, to], parts[g].at[me, s], rs_send_sem.at[g, s, k], rs_recv_sem.at[g, s, k], peer(k)
+        )
+
+    def scatter(g, s):
+        parts[g][me, s] = packs[g][s, me]
+
+        def go(k, c):
+            shard_copy(g, s, k).start()
+            return c
+
+        lax.fori_loop(1, GROUP, go, 0)
+
+    def combine(g):
+        def wait(k, c):
+            for s in range(2):
+                shard_copy(g, s, k).wait()
+            return c
+
+        lax.fori_loop(1, GROUP, wait, 0)
+
+        def add(m, total):
+            for s in range(2):
+                part = parts[g][m, s]
+                total = tuple(
+                    t + part * jnp.broadcast_to(picks[m, s, a:a + 1, 0:1], part.shape)
+                    for a, t in enumerate(total)
+                )
+            return total
+
+        zero = jnp.zeros(parts[g].shape[2:], F32)
+        for a, t in enumerate(lax.fori_loop(0, GROUP, add, (zero,) * 8)):
+            w = denses[g][0].shape[2]
+            denses[g][0][a] = t[:, :w]
+            denses[g][1][a] = t[:, w:]
+
+    def own_copy(g, i):
+        return pltpu.make_async_copy(denses[g][i], gathered[g][i].at[me], own_sem.at[g, i])
+
+    def z_copy(g, i, u):
+        return remote(
+            denses[g][i], gathered[g][i].at[me], z_send.at[g, i, u], z_recv.at[g, i, u], peer(4 * u)
+        )
+
+    def slot(u, k):
+        return lax.bitwise_xor(me, 4 * u + k)
+
+    def plane_copy(g, i, u, way):
+        to = gathered[g][i].at[slot(u, 0)]
+        return remote(
+            denses[g][i] if u == 0 else to, to, plane_send.at[g, i, u, way], plane_recv.at[g, i, u, way],
+            peer(way + 1),
+        )
+
+    def onward_copy(g, i, u, way):
+        at = gathered[g][i].at[slot(u, way + 1), pl.ds(4 * way, 4)]
+        return remote(
+            at, at, plane_send.at[g, i, u, 2 + way], plane_recv.at[g, i, u, 2 + way], peer(2 - way)
+        )
+
+    def swap_copy(g, u):
+        plane = pl.ds(slot(u, 0) // 4 * 4, 4)
+        return remote(
+            gathered[g][1].at[plane], swapped[g].at[plane], swap_send.at[g, u], swap_recv.at[g, u], partner
+        )
+
+    both = [(i, way) for i in range(2) for way in range(2)]
+
+    def gather_first(g):
+        for i in range(2):
+            own_copy(g, i).start()
+            for u in (1, 2, 3):
+                z_copy(g, i, u).start()
+        for i, way in both:
+            plane_copy(g, i, 0, way).start()
+
+    def gather_unit(g, u):
+        for i in range(2):
+            z_copy(g, i, u).wait_recv()
+        for i, way in both:
+            plane_copy(g, i, u, way).start()
+
+    def gather_onward(g, u):
+        for i, way in both:
+            plane_copy(g, i, u, way).wait_recv()
+            onward_copy(g, i, u, way).start()
+
+    def gather_swap(g, u):
+        if u == 0:
+            for i in range(2):
+                own_copy(g, i).wait()
+        for i, way in both:
+            onward_copy(g, i, u, way).wait_recv()
+        swap_copy(g, u).start()
+
+    def gather_end(g):
+        for u in (1, 2, 3):
+            for i in range(2):
+                z_copy(g, i, u).wait_send()
+        for u in range(4):
+            for i, way in both:
+                plane_copy(g, i, u, way).wait_send()
+                onward_copy(g, i, u, way).wait_send()
+            swap_copy(g, u).wait()
 
     def exchange(s):
         return pltpu.make_async_remote_copy(
@@ -148,7 +304,8 @@
         aid = ids[s]
         od_sel = od[aid]
         hs = heads[s]
-        rank_o[s] = nt(od_sel, hs)
+        mine_rk[s, 0:RANK, :] = nt(od_sel, hs)
+        rk_copy(s, 0).start()
         acc[s] = nn(hs, wo[...]) + nn_wide(nt(hs, od_sel), ou[aid])
         exchange(s).start()
         return carry
@@ -212,7 +369,8 @@
         rc, rct = lax.fori_loop(
             0, chunks, chunk, (jnp.zeros((n, RANK), F32), jnp.zeros((RANK, n), F32))
         )
-        rank_c[s] = rct
+        mine_rk[s, RANK:2 * RANK, :] = rct
+        rk_copy(s, 1).start()
         acc[s] += nn_wide(rc, cu[aid])
         send(s)
         return carry
@@ -255,16 +413,25 @@
         back_outer = row[...]
         brc = nt(back_outer, cu_sel).astype(BF16)
         brc_t = nt(cu_sel, back_outer).astype(BF16)
-        t_cu[s] = nn_wide(rank_c[s], back_outer)
+        t_cu = nn_wide(rank_sum(s, 1, RANK), row[:, half])
+        for q in range(4):
+            for h in range(2):
+                pack_e[s, 8 + 2 * q + h, :, 512:640] = t_cu[8 * h:8 * h + 8, 128 * q:128 * q + 128]
         re_t = rank_e[s]
 
         def chunk(c, ranks):
             br, brt = ranks
             at = pl.ds(pl.multiple_of(c * 512, 512), 512)
-            t_cd[s, :, at] = nn(brc_t, hidden[s, :, at])
+            t_cd = nn(brc_t, hidden[s, :, at])
             bh = nt(row[...], wc[at, :]) + nn(brc, cd[aid, :, at])
             bb = (bh * slope[s, :, at].astype(F32)).astype(BF16)
-            t_eu[s, :, at] = nn(re_t, bb)
+            t_eu = nn(re_t, bb)
+            for q in range(2):
+                for h in range(2):
+                    shard = 4 * c + 2 * q + h
+                    part = slice(8 * h, 8 * h + 8), slice(256 * q, 256 * q + 256)
+                    pack_e[s, shard, :, 0:256] = t_eu[part]
+                    pack_e[s, shard, :, 256:512] = t_cd[part]
             acc[s] += nt(bb, we[:, at])
             eu_sel = eu[aid, :, at]
             return br + nt(bb, eu_sel), brt + nt(eu_sel, bb)
@@ -272,16 +439,63 @@
         br, brt = lax.fori_loop(
             0, chunks, chunk, (jnp.zeros((n, RANK), F32), jnp.zeros((RANK, n), F32))
         )
+        mine_rk[s, 2 * RANK:3 * RANK, :] = brt
+        rk_copy(s, 2).start()
         acc[s] += nn_wide(br, ed[aid])
         send(s)
-        inner = (xhat[s] * g1[...] + b1[...]).astype(BF16)
-        t_ed[s] = nn_wide(brt, inner)
         return carry
 
     load_cot.wait()
     lax.fori_loop(0, 2, stage3, 0)
 
+    def early(s, carry):
+        inner = (xhat[s, :, half] * g1[:, half] + b1[:, half]).astype(BF16)
+        t_ed = nn_wide(rank_sum(s, 2, RANK), inner)
+        for q in range(4):
+            for h in range(2):
+                pack_e[s, 2 * q + h, :, 512:640] = t_ed[8 * h:8 * h + 8, 128 * q:128 * q + 128]
+        scatter(0, s)
+        return carry
+
+    lax.fori_loop(0, 2, early, 0)
+
     d_out, d_q, d_k, d_v, dq_t = 0, 1, 2, 3, 4
+
+    def put_late(s, t, up, down):
+        for q in range(2):
+            for h in range(2):
+                part = slice(8 * h, 8 * h + 8), slice(256 * q, 256 * q + 256)
+                if up is not None:
+                    pack_l[s, 4 * t + 2 * q + h, :, 0:256] = up[part]
+                if down is not None:
+                    pack_l[s, 4 * t + 2 * q + h, :, 256:512] = down[part]
+
+    def between(s, hp):
+        def at(s_, hp_, f):
+            @pl.when(jnp.logical_and(s == s_, hp == hp_))
+            def _():
+                f()
+
+        def begin():
+            combine(0)
+            gather_first(0)
+
+        def step(u):
+            def f():
+                gather_unit(0, u)
+                gather_onward(0, u - 1)
+            return f
+
+        at(0, 3, begin)
+        at(1, 0, step(1))
+        at(1, 1, step(2))
+        at(1, 3, step(3))
+
+    def wait_picks(k, c):
+        pick_copy(k).wait()
+        return c
+
+    lax.fori_loop(1, GROUP, wait_picks, 0)
 
     def stage4(s, carry):
         aid = ids[s]
@@ -305,9 +519,8 @@
         back_branch = row[...]
         bro = nt(back_branch, ou_sel).astype(BF16)
         bro_t = nt(ou_sel, back_branch).astype(BF16)
-        t_ou[s] = nn_wide(rank_o[s], back_branch)
         hs = heads[s]
-        t_od[s] = nn(bro_t, hs)
+        put_late(s, 3, nn(bro_t, hs), nn_wide(rank_sum(s, 0, RANK), row[:, half]))
         d_heads = (nt(back_branch, wo[...]) + nn(bro, od_sel)).astype(BF16)
         work[d_out] = d_heads
         pick = (
@@ -315,10 +528,7 @@
             == lax.broadcasted_iota(jnp.int32, (RANK, heads_half), 0)
         ).astype(BF16)
         hi, lo = split(d_heads.astype(F32) * hs.astype(F32))
-        lcol[0:RANK, 0:128] = jnp.zeros((RANK, 128), F32)
-        dots = nt(pick, hi) + nt(pick, lo)
-        drow = rank_o.at[s]
-        drow[...] = dots
+        drow[...] = nt(pick, hi) + nt(pick, lo)
 
         def pair(hp, c):
             at = pl.ds(pl.multiple_of(hp * 128, 128), 128)
@@ -342,17 +552,31 @@
                 work[dq_t, pl.ds(pl.multiple_of(h * HEAD_WIDTH, HEAD_WIDTH), HEAD_WIDTH), :] = dqt.astype(BF16)
             work[d_k, :, at] = jnp.where(low_half, dk[0], dk[1]).astype(BF16)
             work[d_v, :, at] = jnp.where(low_half, dv[0], dv[1]).astype(BF16)
+            between(s, hp)
             return c
 
         lax.fori_loop(0, pairs, pair, 0)
         work[d_q] = work[dq_t].T
+
+        def terms(p, c):
+            dp_ = work[1 + p]
+            put_late(s, p, nn(rank_t[s, p], dp_), None)
+            mine_rk[s, pl.ds(pl.multiple_of((3 + p) * RANK, RANK), RANK), :] = nt(utab[p, aid], dp_)
+            return c
+
+        lax.fori_loop(0, 3, terms, 0)
+        rk_copy(s, 3).start()
+        hi, lo = split(rank_sum(s, 3, 3 * RANK))
+        xs = x[s, :, half]
+        t_d = nn(hi, xs) + nn(lo, xs)
+        for p in range(3):
+            put_late(s, p, None, t_d[RANK * p:RANK * p + RANK, :])
+        scatter(1, s)
 
         def project(p, c):
             dp_ = work[1 + p]
             u_sel = utab[p, aid]
             d_sel = dtab[p, aid]
-            t_u[s, p] = nn(rank_t[s, p], dp_)
-            t_d[s, p] = nn_wide(nt(u_sel, dp_), x[s])
             acc[s] += nt(dp_, wp[p]) + nn_wide(nt(dp_, u_sel), d_sel)
             return c
 
@@ -362,6 +586,8 @@
 
     lax.fori_loop(0, 2, stage4, 0)
 
+    gather_onward(0, 3)
+
     def stage5(s, carry):
         exchange(s).wait()
         put_out(s).wait()
@@ -376,8 +602,94 @@
         return carry
 
     lax.fori_loop(0, 2, stage5, 0)
+    for u in range(4):
+        gather_swap(0, u)
+    combine(1)
+    gather_first(1)
+    for u in (1, 2, 3):
+        gather_unit(1, u)
+        gather_onward(1, u - 1)
+    gather_onward(1, 3)
+    for u in range(4):
+        gather_swap(1, u)
+    gather_end(0)
+    gather_end(1)
     put_grad(0).wait()
     put_grad(1).wait()
+
+
+def place_kernel(*refs):
+    src, dst, src_v, dst_v = refs[:8], refs[8:22], refs[22:30], refs[30:42]
+    in_sem, out_sem = refs[42:]
+    core = lax.axis_index("tensor")
+    loads = [pltpu.make_async_copy(a, b, in_sem.at[i]) for i, (a, b) in enumerate(zip(src, src_v))]
+    for cp in loads:
+        cp.start()
+    ends = []
+
+    def store(v, i):
+        cp = pltpu.make_async_copy(v, dst[i], out_sem.at[i])
+        cp.start()
+        ends.append(cp)
+
+    qd, qu, kd, ku, vd, vu, od, ou, ed, eu, cd, cu = range(12)
+    up, down, low = (qu, ku, vu, od), (qd, kd, vd, ou), (ed, cu)
+    geu, ger, glu, glr, her, hlr = src_v[:6]
+
+    def lanes(side, width, i):
+        return pl.ds(pl.multiple_of(side * 512 + width * i, 128), width)
+
+    def rows(n):
+        return slice(8 * (n % 2), 8 * (n % 2) + 8)
+
+    loads[0].wait()
+    for n in range(GROUP):
+        at = slice(256 * (n // 2), 256 * (n // 2) + 256)
+        dst_v[eu][:, rows(n), at] = geu[n, :, :, 0:256]
+        dst_v[cd][:, rows(n), at] = geu[n, :, :, 256:512]
+    store(dst_v[eu], 2 + eu)
+    store(dst_v[cd], 2 + cd)
+    for i in (1, 4):
+        loads[i].wait()
+    for n in range(GROUP):
+        v = dst_v[low[n // 8]]
+        v[:, rows(n), lanes(core, 128, n % 8 // 2)] = ger[n]
+        v[:, rows(n), lanes(1 - core, 128, n % 8 // 2)] = her[n]
+    store(dst_v[ed], 2 + ed)
+    store(dst_v[cu], 2 + cu)
+    for i in (2, 3, 5):
+        loads[i].wait()
+    for t in range(4):
+        for n in range(4 * t, 4 * t + 4):
+            q = n % 4 // 2
+            dst_v[up[t]][:, rows(n), 256 * q:256 * q + 256] = glu[n]
+            dst_v[down[t]][:, rows(n), lanes(core, 256, q)] = glr[n]
+            dst_v[down[t]][:, rows(n), lanes(1 - core, 256, q)] = hlr[n]
+        store(dst_v[up[t]], 2 + up[t])
+        store(dst_v[down[t]], 2 + down[t])
+    for i in range(2):
+        loads[6 + i].wait()
+        store(src_v[6 + i], i)
+    for cp in ends:
+        cp.wait()
+
+
+def place(out, grad, tables, hw, f):
+    s, n, d = out.shape
+    hbm = pl.BlockSpec(memory_space=pl.ANY)
+    widths = (d, hw, d, hw, d, hw, hw, d, d, f, f, d)
+    args = (*tables, out, grad)
+    return pl.pallas_call(
+        place_kernel,
+        out_shape=[jax.ShapeDtypeStruct((s, n, d), BF16)] * 2
+        + [jax.ShapeDtypeStruct((8, RANK, w), F32) for w in widths],
+        in_specs=[hbm] * 8,
+        out_specs=[hbm] * 14,
+        scratch_shapes=[pltpu.VMEM(a.shape, a.dtype) for a in args]
+        + [pltpu.VMEM((8, RANK, w), F32) for w in widths]
+        + [pltpu.SemaphoreType.DMA((8,)), pltpu.SemaphoreType.DMA((14,))],
+        compiler_params=pltpu.CompilerParams(vmem_limit_bytes=40 * 1024 * 1024),
+    )(*args)
 
 
 def layer(ids, seg, x, cot, wq, wk, wv, wo, we, wc, g1, b1, g2, b2, *tables):
@@ -392,13 +704,13 @@
         layer_kernel,
         out_shape=(
             sds((s, n, d), BF16), sds((s, n, d), BF16),
-            sds((s, 3, RANK, hw), F32), sds((s, 3, RANK, d), F32), sds((s, RANK, hw), F32),
-            sds((s, RANK, d), F32), sds((s, RANK, f), F32), sds((s, RANK, f), F32),
-            sds((s, RANK, d), F32), sds((s, RANK, d), F32),
+            sds((GROUP, 8, 8, 512), F32), sds((GROUP, 8, 8, 128), F32),
+            sds((GROUP, 8, 8, 256), F32), sds((GROUP, 8, 8, 256), F32),
+            sds((GROUP, 8, 8, 128), F32), sds((GROUP, 8, 8, 256), F32),
         ),
         in_specs=[sm, vm, hbm, hbm, hbm, hbm, hbm, hbm, hbm, hbm, vm, vm, vm, vm]
         + [hbm] * 6 + [vm] * 6,
-        out_specs=(hbm, hbm) + (vm,) * 8,
+        out_specs=(hbm,) * 8,
         scratch_shapes=[
             pltpu.VMEM((s, n, d), BF16),
             pltpu.VMEM((s, n, d), BF16),
@@ -422,15 +734,39 @@
             pltpu.VMEM((5, n, hw), BF16),
             pltpu.VMEM((n, 128), F32),
             pltpu.VMEM((s, 3, RANK, n), BF16),
-            pltpu.VMEM((s, RANK, n), F32),
             pltpu.VMEM((s, RANK, n), BF16),
-            pltpu.VMEM((s, RANK, n), F32),
+            pltpu.VMEM((RANK, n), F32),
+            pltpu.VMEM((s, 6 * RANK, n), F32),
+            pltpu.VMEM((s, 6 * RANK, n), F32),
             pltpu.VMEM((s, n, d), BF16),
+            pltpu.VMEM((s, 8, 128), F32),
+            pltpu.VMEM((GROUP, s, 8, 128), F32),
+            pltpu.VMEM((s, GROUP, 8, EARLY), F32),
+            pltpu.VMEM((s, GROUP, 8, LATE), F32),
+            pltpu.VMEM((GROUP, s, 8, EARLY), F32),
+            pltpu.VMEM((GROUP, s, 8, LATE), F32),
+            pltpu.VMEM((8, 8, 512), F32),
+            pltpu.VMEM((8, 8, 128), F32),
+            pltpu.VMEM((8, 8, 256), F32),
+            pltpu.VMEM((8, 8, 256), F32),
             pltpu.SemaphoreType.DMA((14,)),
             pltpu.SemaphoreType.DMA((2,)),
             pltpu.SemaphoreType.DMA((2,)),
             pltpu.SemaphoreType.DMA((2,)),
             pltpu.SemaphoreType.REGULAR((2,)),
+            pltpu.SemaphoreType.DMA((2, 4)),
+            pltpu.SemaphoreType.DMA((2, 4)),
+            pltpu.SemaphoreType.DMA((GROUP,)),
+            pltpu.SemaphoreType.DMA((GROUP,)),
+            pltpu.SemaphoreType.DMA((2, 2, GROUP)),
+            pltpu.SemaphoreType.DMA((2, 2, GROUP)),
+            pltpu.SemaphoreType.DMA((2, 2, 4)),
+            pltpu.SemaphoreType.DMA((2, 2, 4)),
+            pltpu.SemaphoreType.DMA((2, 2, 4, 4)),
+            pltpu.SemaphoreType.DMA((2, 2, 4, 4)),
+            pltpu.SemaphoreType.DMA((2, 2)),
+            pltpu.SemaphoreType.DMA((2, 4)),
+            pltpu.SemaphoreType.DMA((2, 4)),
         ],
         compiler_params=pltpu.CompilerParams(
             collective_id=0, has_side_effects=True, vmem_limit_bytes=63 * 1024 * 1024
@@ -448,7 +784,7 @@
     width = tokens.shape[1]
     turn = lambda t: jnp.swapaxes(t, 1, 2)
     line = lambda v: v.reshape(1, -1)
-    out, grad, t_u, t_d, t_od, t_ou, t_eu, t_cd, t_ed, t_cu = layer(
+    out, grad, *tables = layer(
         adapter_ids, segment_ids.astype(F32),
         tokens.reshape(seqs, length, width), cotangent.reshape(seqs, length, width),
         query_weight, key_weight, value_weight, output_weight, expand_weight, contract_weight,
@@ -456,18 +792,15 @@
         turn(query_down), turn(key_down), turn(value_down), query_up, key_up, value_up,
         turn(output_down), output_up, turn(expand_down), expand_up, turn(contract_down), contract_up,
     )
-    selector = (
-        adapter_ids[:, None] == jnp.arange(query_down.shape[0], dtype=jnp.int32)[None, :]
-    ).astype(F32)
-    spread = lambda t: jnp.einsum("se,s...->e...", selector, t, precision=lax.Precision.HIGHEST)
-    both = lax.psum((spread(t_d), spread(t_ou), spread(t_ed), spread(t_cu)), ("dp", "tensor"))
-    one = lax.psum((spread(t_u), spread(t_od), spread(t_eu), spread(t_cd)), "dp")
-    g_d, g_ou, g_ed, g_cu = both
-    g_u, g_od, g_eu, g_cd = one
+    out, grad, *tables = place(out, grad, tables, query_weight.shape[1], expand_weight.shape[1])
+    count = lax.axis_size("dp")
+    if count > GROUP:
+        across = [list(range(i, count, GROUP)) for i in range(GROUP)]
+        tables = lax.psum(tuple(tables), "dp", axis_index_groups=across)
+    qd, qu, kd, ku, vd, vu, od, ou, ed, eu, cd, cu = tables
     return (
         out.reshape(tokens.shape), grad.reshape(tokens.shape),
-        turn(g_d[:, 0]), g_u[:, 0], turn(g_d[:, 1]), g_u[:, 1], turn(g_d[:, 2]), g_u[:, 2],
-        turn(g_od), g_ou, turn(g_ed), g_eu, turn(g_cd), g_cu,
+        turn(qd), qu, turn(kd), ku, turn(vd), vu, turn(od), ou, turn(ed), eu, turn(cd), cu,
     )
 
 

time: 448 us -> 183 us (0.41)
  waiting for transfers between devices: 282 us -> 0 us
  Pallas kernels: 115 us -> 170 us
  matrix products: 15.3 us -> 0 us
  between operations: 14.1 us -> 0.83 us
  local copies, waits for them, and re-layouts: 19.6 us -> 10.5 us
    psum x2 -> x0, waiting for transfers between devices: 282 us -> none  [the longest x1 147 us: on_device(): lax.psum((spread(t_u), spread(t_od), spread(t_eu), spread(t_cd)), 'dp')]
    pallas_call x1, Pallas kernels: 115 us -> 165 us  [layer(): pl.pallas_call(layer_kernel, out_shape=(sds((s, n, d), BF16), sds((s, n,...]
    dot_general x8 -> x0, matrix products: 15.3 us -> none  [on_device(): jnp.einsum('se,s...->e...', selector, t, precision=lax.Precision.HIGHEST)]
    unnamed x42 -> x16, local copies, waits for them, and re-layouts: 16.9 us -> 10.5 us
    pallas_call x0 -> x1, Pallas kernels: none -> 4.92 us  [place(): pl.pallas_call(place_kernel, out_shape=[jax.ShapeDtypeStruct((s, n, d), B...]
  transfers between devices with their start and end apart: 2 -> 0, of which waited for: 2 -> 0; matrix products, arithmetic and copies ran while one was open for 3% -> 0% of each run, Pallas kernels for 0% -> 0%
where the time goes in v2:
time: 183 us
  Pallas kernels  170 us (93%)
  local copies, waits for them, and re-layouts  10.5 us (6%)
    pallas_call x1, Pallas kernels, layer(): pl.pallas_call(layer_kernel, out_shape=(sds((s, n, d), BF16), sds((s, n,...  165 us
    unnamed x16, local copies, waits for them, and re-layouts  10.5 us
    pallas_call x1, Pallas kernels, place(): pl.pallas_call(place_kernel, out_shape=[jax.ShapeDtypeStruct((s, n, d), B...  4.92 us

profile of v2, /device:TPU:0, one launch (start us, length us, event | category | flops | bytes accessed | tf_op | source)
XLA Modules:
  0.0 183.0 jit_solution(7051656248973970000)
XLA Ops:
  0.6 1.3 convert_element_type.3.seg
  1.9 165.4 %shard_map.353 = (bf16[2,512,1024]{2,1,0:T(8,128)(2,1)}, bf16[2,512,1024]{2,1,0:T(8,128)(2,1)}, f32[16,8,8,512]{3,2,1,0:T(8,128)}, f32[16,8,8,128]{3,2,1,0:T(8,1...) custom-call(s32[2]{0:T(128)} %ids.1, ...), custom_call_target="tpu_custom_call" | custom-call | tf_op jit(solution)/shard_map/pallas_call | solution.py:703
  167.4 0.0 copy-start
  167.4 1.6 copy-done
  169.0 0.0 copy-start.1
  169.0 1.6 copy-done.1
  170.6 0.0 copy-start.2
  170.6 1.6 copy-done.2
  172.1 0.0 copy-start.3
  172.1 1.2 copy-done.3
  173.4 0.0 copy-start.4
  173.4 1.2 copy-done.4
  174.6 0.0 copy-start.5
  174.6 1.2 copy-done.5
  175.8 0.0 copy-start.6
  175.8 1.0 copy-done.6
  176.9 0.0 copy-start.7
  176.9 1.0 copy-done.7
  177.9 4.9 %shard_map.354 = (bf16[2,512,1024]{2,1,0:T(8,128)(2,1)}, bf16[2,512,1024]{2,1,0:T(8,128)(2,1)}, f32[8,16,1024]{2,1,0:T(8,128)}, f32[8,16,512]{2,1,0:T(8,128)}, f...) custom-call(f32[16,8,8,512]{3,2,1,0:T(8,128)S(1)} %copy-done.2, ...), custom_call_target="tpu_custom_call" | custom-call | tf_op jit(solution)/shard_map/pallas_call | solution.py:682
Async XLA Ops:
  167.4 1.6 copy-start
  169.0 1.6 copy-start.1
  170.6 1.6 copy-start.2
  172.1 1.2 copy-start.3
  173.4 1.2 copy-start.4
  174.6 1.2 copy-start.5
  175.8 1.0 copy-start.6
  176.9 1.0 copy-start.7

commit v3 on v2

--- a/solution.py
+++ b/solution.py
@@ -11,7 +11,7 @@
 F32 = jnp.float32
 BF16 = jnp.bfloat16
 EPS = 1e-05
-ROWS = 64
+ROWS = 128
 GROUP = 16
 EARLY, LATE = 640, 512
 
@@ -50,7 +50,7 @@
     qd, kd, vd, qu, ku, vu, od, ou, ed, eu, cd, cu,
     out_hbm, grad_hbm, geu, ger, glu, glr, her, hlr,
     x, cot, wp, wo, we, wc, dtab, utab, qkv, heads, bias, lse, xhat, rstd, hidden, slope, acc, recv,
-    row, work, lcol, rank_t, rank_e, drow, mine_rk, their_rk, stage_out,
+    row, d_heads, d_qkv, dq_t, u_cat, d_cat, lcol, rank_t, rank_e, drow, mine_rk, their_rk, stage_out,
     pick_mine, picks, pack_e, pack_l, rs_e, rs_l, dense_eu, dense_er, dense_lu, dense_lr,
     load_sem, send_sem, recv_sem, out_sem, credit, rk_send, rk_recv, pick_send, pick_recv,
     rs_send_sem, rs_recv_sem, z_send, z_recv, plane_send, plane_recv, own_sem, swap_send, swap_recv,
@@ -71,7 +71,7 @@
     loads = [load(0, x_hbm, x)]
     tabs = []
     for i, (w, d, u) in enumerate(((wq, qd, qu), (wk, kd, ku), (wv, vd, vu))):
-        tabs.append(load(1 + i, w, wp.at[i]))
+        tabs.append(load(1 + i, w, wp.at[:, pl.ds(512 * i, 512)]))
         tabs.append(load(4 + i, d, dtab.at[i]))
         tabs.append(load(7 + i, u, utab.at[i]))
     load_wo = load(10, wo_hbm, wo)
@@ -246,8 +246,8 @@
         exchange(s).start()
 
     n = x.shape[1]
-    heads_half = heads.shape[2]
-    pairs = heads_half // 128
+    hw = heads.shape[2]
+    pairs = hw // 128
     chunks = hidden.shape[2] // 512
     lane = lax.broadcasted_iota(jnp.int32, (n, 128), 1)
     low_half = lane < HEAD_WIDTH
@@ -255,21 +255,45 @@
     for cp in loads + tabs:
         cp.wait()
 
+    u_cat[...] = jnp.zeros_like(u_cat)
+    d_cat[...] = jnp.zeros_like(d_cat)
+
+    def stack_tables(aid):
+        for p in range(3):
+            for r in (0, 64):
+                rows = slice(r + RANK * p, r + RANK * p + RANK)
+                d_cat[rows, :] = dtab[p, aid]
+                u_cat[rows, hw * p:hw * p + hw] = utab[p, aid]
+
+    def twice(t):
+        return jnp.concatenate([t, t], axis=0)
+
+    def wide(v, at):
+        hi = v.astype(BF16).astype(F32)
+        return jnp.where(lax.broadcasted_iota(jnp.int32, v.shape, 1) < at, hi, v - hi).astype(BF16)
+
+    def term(v, right):
+        k = v.shape[0]
+        hi, lo = split(v)
+        both_parts = nn(jnp.concatenate([hi, lo], axis=0), right)
+        return both_parts[:k] + both_parts[k:]
+
     def stage1(s, carry):
         aid = ids[s]
-        xs = x.at[s]
         seg_row = seg[pl.ds(s, 1), :]
         seg_col = jnp.broadcast_to(seg_row, (128, n)).T
         for j in range(n // 128):
             same = seg_col == seg_row[:, j * 128:(j + 1) * 128]
             bias[s, :, j * 128:(j + 1) * 128] = jnp.where(same, 0.0, -1e30)
+        stack_tables(aid)
+        rank = jnp.where(lane < 64, nt(x[s], d_cat[...]), 0.0)
+        rank_t[s] = rank.T[0:3 * RANK, :].astype(BF16)
+        rank = rank.astype(BF16)
 
         def project(p, c):
-            d_sel = dtab[p, aid]
-            rank = nt(xs[...], d_sel).astype(BF16)
-            rank_t[s, p] = nt(d_sel, xs[...]).astype(BF16)
+            at = pl.ds(pl.multiple_of(p * hw, hw), hw)
             scale = jnp.where(p == 0, 0.125, 1.0)
-            qkv[s, p] = ((nn(xs[...], wp[p]) + nn(rank, utab[p, aid])) * scale).astype(BF16)
+            qkv[s, p] = ((nn(x[s], wp[:, at]) + nn(rank, u_cat[:, at])) * scale).astype(BF16)
             return c
 
         lax.fori_loop(0, 3, project, 0)
@@ -288,9 +312,9 @@
                     score = nt(jnp.where(mine, q2, jnp.zeros_like(q2)), k2) + bias[s, rows, :]
                     top = jnp.max(score, axis=1, keepdims=True)
                     e = jnp.exp(score - top).astype(BF16)
-                    both = nn(e, v2)
-                    total = both[:, 128:]
-                    outs.append(both[:, :128] / total)
+                    parts_ = nn(e, v2)
+                    total = parts_[:, 128:]
+                    outs.append(parts_[:, :128] / total)
                     old = lcol[rows, :]
                     lcol[rows, :] = jnp.where(ln == 2 * hp + j, top + jnp.log(total), old)
                 heads[s, rows, at] = jnp.where(ln < HEAD_WIDTH, outs[0], outs[1]).astype(BF16)
@@ -298,29 +322,20 @@
 
         lax.fori_loop(0, pairs, pair, 0)
         lse[s] = lcol[...].T[:lse.shape[1], :]
-        return carry
-
-    def stage1_out(s, carry):
-        aid = ids[s]
-        od_sel = od[aid]
-        hs = heads[s]
-        mine_rk[s, 0:RANK, :] = nt(od_sel, hs)
-        rk_copy(s, 0).start()
-        acc[s] = nn(hs, wo[...]) + nn_wide(nt(hs, od_sel), ou[aid])
-        exchange(s).start()
-        return carry
-
-    def both1(s, carry):
-        stage1(s, carry)
 
         @pl.when(s == 0)
         def _():
             load_wo.wait()
 
-        stage1_out(s, carry)
+        hs = heads[s]
+        ro = nt(hs, twice(od[aid]))
+        mine_rk[s, 0:RANK, :] = ro.T[0:RANK, :]
+        rk_copy(s, 0).start()
+        acc[s] = nn(hs, wo[...]) + nn(wide(ro, RANK), twice(ou[aid]))
+        exchange(s).start()
         return carry
 
-    lax.fori_loop(0, 2, both1, 0)
+    lax.fori_loop(0, 2, stage1, 0)
 
     def stage2(s, carry):
         aid = ids[s]
@@ -340,38 +355,30 @@
 
         lax.fori_loop(0, n // ROWS, norm, 0)
         taken(s)
-        ed_sel = ed[aid]
-        inner = row[...]
-        rank = nt(inner, ed_sel).astype(BF16)
-        rank_e[s] = nt(ed_sel, inner).astype(BF16)
-
-        def chunk(c, ranks):
-            rc, rct = ranks
-            at = pl.ds(pl.multiple_of(c * 512, 512), 512)
-            before = nn(row[...], we[:, at]) + nn(rank, eu[aid, :, at])
+        rank = nt(row[...], ed[aid])
+        rank_e[s] = rank.T.astype(BF16)
+        rank = rank.astype(BF16)
+
+        def expand(c):
+            at = slice(512 * c, 512 * c + 512)
+            return nn(row[...], we[:, at]) + nn(rank, eu[aid, :, at])
+
+        before = expand(0)
+        for c in range(chunks):
+            after = expand(c + 1) if c + 1 < chunks else None
+            at = slice(512 * c, 512 * c + 512)
             hid, sl = gelu_parts(before)
-            hid = hid.astype(BF16)
-            hidden[s, :, at] = hid
+            hidden[s, :, at] = hid.astype(BF16)
             slope[s, :, at] = sl.astype(BF16)
-            cd_sel = cd[aid, :, at]
-            part = nn(hid, wc[at, :])
-
-            @pl.when(c == 0)
-            def _():
-                acc[s] = part
-
-            @pl.when(c > 0)
-            def _():
-                acc[s] += part
-
-            return rc + nt(hid, cd_sel), rct + nt(cd_sel, hid)
-
-        rc, rct = lax.fori_loop(
-            0, chunks, chunk, (jnp.zeros((n, RANK), F32), jnp.zeros((RANK, n), F32))
-        )
-        mine_rk[s, RANK:2 * RANK, :] = rct
+            before = after
+        rc = nt(hidden[s], twice(cd[aid]))
+        mine_rk[s, RANK:2 * RANK, :] = rc.T[0:RANK, :]
         rk_copy(s, 1).start()
-        acc[s] += nn_wide(rc, cu[aid])
+        rc = wide(rc, RANK)
+        cu2 = twice(cu[aid])
+        for c in range(2):
+            at = slice(512 * c, 512 * c + 512)
+            acc[s, :, at] = nn(hidden[s], wc[:, at]) + nn(rc, cu2[:, at])
         send(s)
         return carry
 
@@ -409,39 +416,41 @@
         lax.fori_loop(0, n // ROWS, norm, 0)
         taken(s)
         put_out(s).start()
-        cu_sel = cu[aid]
-        back_outer = row[...]
-        brc = nt(back_outer, cu_sel).astype(BF16)
-        brc_t = nt(cu_sel, back_outer).astype(BF16)
-        t_cu = nn_wide(rank_sum(s, 1, RANK), row[:, half])
+        brc = nt(row[...], cu[aid])
+        brc_t = brc.T.astype(BF16)
+        brc = brc.astype(BF16)
+        t_cu = term(rank_sum(s, 1, RANK), row[:, half])
         for q in range(4):
             for h in range(2):
                 pack_e[s, 8 + 2 * q + h, :, 512:640] = t_cu[8 * h:8 * h + 8, 128 * q:128 * q + 128]
         re_t = rank_e[s]
 
-        def chunk(c, ranks):
-            br, brt = ranks
-            at = pl.ds(pl.multiple_of(c * 512, 512), 512)
-            t_cd = nn(brc_t, hidden[s, :, at])
-            bh = nt(row[...], wc[at, :]) + nn(brc, cd[aid, :, at])
-            bb = (bh * slope[s, :, at].astype(F32)).astype(BF16)
-            t_eu = nn(re_t, bb)
+        def early_parts(c, t, lanes):
             for q in range(2):
                 for h in range(2):
-                    shard = 4 * c + 2 * q + h
-                    part = slice(8 * h, 8 * h + 8), slice(256 * q, 256 * q + 256)
-                    pack_e[s, shard, :, 0:256] = t_eu[part]
-                    pack_e[s, shard, :, 256:512] = t_cd[part]
-            acc[s] += nt(bb, we[:, at])
-            eu_sel = eu[aid, :, at]
-            return br + nt(bb, eu_sel), brt + nt(eu_sel, bb)
-
-        br, brt = lax.fori_loop(
-            0, chunks, chunk, (jnp.zeros((n, RANK), F32), jnp.zeros((RANK, n), F32))
-        )
-        mine_rk[s, 2 * RANK:3 * RANK, :] = brt
+                    pack_e[s, 4 * c + 2 * q + h, :, lanes] = t[8 * h:8 * h + 8, 256 * q:256 * q + 256]
+
+        def contract_back(c):
+            at = slice(512 * c, 512 * c + 512)
+            return nt(row[...], wc[at, :]) + nn(brc, cd[aid, :, at])
+
+        bh = contract_back(0)
+        for c in range(chunks):
+            after = contract_back(c + 1) if c + 1 < chunks else None
+            at = slice(512 * c, 512 * c + 512)
+            early_parts(c, nn(brc_t, hidden[s, :, at]), slice(256, 512))
+            bb = (bh * slope[s, :, at].astype(F32)).astype(BF16)
+            slope[s, :, at] = bb
+            early_parts(c, nn(re_t, bb), slice(0, 256))
+            bh = after
+        br = nt(slope[s], twice(eu[aid]))
+        mine_rk[s, 2 * RANK:3 * RANK, :] = br.T[0:RANK, :]
         rk_copy(s, 2).start()
-        acc[s] += nn_wide(br, ed[aid])
+        br = wide(br, RANK)
+        ed2 = twice(ed[aid])
+        for c in range(2):
+            at = slice(512 * c, 512 * c + 512)
+            acc[s, :, at] += nt(slope[s], we[at, :]) + nn(br, ed2[:, at])
         send(s)
         return carry
 
@@ -450,7 +459,7 @@
 
     def early(s, carry):
         inner = (xhat[s, :, half] * g1[:, half] + b1[:, half]).astype(BF16)
-        t_ed = nn_wide(rank_sum(s, 2, RANK), inner)
+        t_ed = term(rank_sum(s, 2, RANK), inner)
         for q in range(4):
             for h in range(2):
                 pack_e[s, 2 * q + h, :, 512:640] = t_ed[8 * h:8 * h + 8, 128 * q:128 * q + 128]
@@ -458,8 +467,6 @@
         return carry
 
     lax.fori_loop(0, 2, early, 0)
-
-    d_out, d_q, d_k, d_v, dq_t = 0, 1, 2, 3, 4
 
     def put_late(s, t, up, down):
         for q in range(2):
@@ -514,20 +521,17 @@
 
         lax.fori_loop(0, n // ROWS, norm, 0)
         taken(s)
-        ou_sel = ou[aid]
-        od_sel = od[aid]
-        back_branch = row[...]
-        bro = nt(back_branch, ou_sel).astype(BF16)
-        bro_t = nt(ou_sel, back_branch).astype(BF16)
         hs = heads[s]
-        put_late(s, 3, nn(bro_t, hs), nn_wide(rank_sum(s, 0, RANK), row[:, half]))
-        d_heads = (nt(back_branch, wo[...]) + nn(bro, od_sel)).astype(BF16)
-        work[d_out] = d_heads
+        bro = nt(row[...], ou[aid])
+        put_late(
+            s, 3, nn(bro.T.astype(BF16), hs), term(rank_sum(s, 0, RANK), row[:, half])
+        )
+        d_heads[...] = (nt(row[...], wo[...]) + nn(bro.astype(BF16), od[aid])).astype(BF16)
         pick = (
-            lax.broadcasted_iota(jnp.int32, (RANK, heads_half), 1) // HEAD_WIDTH
-            == lax.broadcasted_iota(jnp.int32, (RANK, heads_half), 0)
+            lax.broadcasted_iota(jnp.int32, (RANK, hw), 1) // HEAD_WIDTH
+            == lax.broadcasted_iota(jnp.int32, (RANK, hw), 0)
         ).astype(BF16)
-        hi, lo = split(d_heads.astype(F32) * hs.astype(F32))
+        hi, lo = split(d_heads[...].astype(F32) * hs.astype(F32))
         drow[...] = nt(pick, hi) + nt(pick, lo)
 
         def pair(hp, c):
@@ -535,7 +539,7 @@
             q2 = qkv[s, 0, :, at]
             k2 = qkv[s, 1, :, at]
             v2 = qkv[s, 2, :, at]
-            do2 = work[d_out, :, at]
+            do2 = d_heads[:, at]
             k2t = k2.T
             zero = jnp.zeros_like(k2)
             dk, dv = [], []
@@ -549,38 +553,31 @@
                 dv.append(nn(pt.astype(BF16), do2))
                 dk.append(nn(dst, q2))
                 dqt = nn(k2t[j * HEAD_WIDTH:(j + 1) * HEAD_WIDTH, :], dst) * 0.125
-                work[dq_t, pl.ds(pl.multiple_of(h * HEAD_WIDTH, HEAD_WIDTH), HEAD_WIDTH), :] = dqt.astype(BF16)
-            work[d_k, :, at] = jnp.where(low_half, dk[0], dk[1]).astype(BF16)
-            work[d_v, :, at] = jnp.where(low_half, dv[0], dv[1]).astype(BF16)
+                dq_t[pl.ds(pl.multiple_of(h * HEAD_WIDTH, HEAD_WIDTH), HEAD_WIDTH), :] = dqt.astype(BF16)
+            to = pl.multiple_of(hp * 128, 128)
+            d_qkv[:, pl.ds(hw + to, 128)] = jnp.where(low_half, dk[0], dk[1]).astype(BF16)
+            d_qkv[:, pl.ds(2 * hw + to, 128)] = jnp.where(low_half, dv[0], dv[1]).astype(BF16)
             between(s, hp)
             return c
 
         lax.fori_loop(0, pairs, pair, 0)
-        work[d_q] = work[dq_t].T
-
-        def terms(p, c):
-            dp_ = work[1 + p]
-            put_late(s, p, nn(rank_t[s, p], dp_), None)
-            mine_rk[s, pl.ds(pl.multiple_of((3 + p) * RANK, RANK), RANK), :] = nt(utab[p, aid], dp_)
-            return c
-
-        lax.fori_loop(0, 3, terms, 0)
+        d_qkv[:, 0:hw] = dq_t[...].T
+        stack_tables(aid)
+        br = nt(d_qkv[...], u_cat[...])
+        mine_rk[s, 3 * RANK:6 * RANK, :] = br.T[0:3 * RANK, :]
         rk_copy(s, 3).start()
-        hi, lo = split(rank_sum(s, 3, 3 * RANK))
-        xs = x[s, :, half]
-        t_d = nn(hi, xs) + nn(lo, xs)
+        br = wide(br, 64)
+        for p in range(3):
+            put_late(
+                s, p, nn(rank_t[s, RANK * p:RANK * p + RANK, :], d_qkv[:, hw * p:hw * p + hw]), None
+            )
+        t_d = term(rank_sum(s, 3, 3 * RANK), x[s, :, half])
         for p in range(3):
             put_late(s, p, None, t_d[RANK * p:RANK * p + RANK, :])
         scatter(1, s)
-
-        def project(p, c):
-            dp_ = work[1 + p]
-            u_sel = utab[p, aid]
-            d_sel = dtab[p, aid]
-            acc[s] += nt(dp_, wp[p]) + nn_wide(nt(dp_, u_sel), d_sel)
-            return c
-
-        lax.fori_loop(0, 3, project, 0)
+        for c in range(2):
+            at = slice(512 * c, 512 * c + 512)
+            acc[s, :, at] += nt(d_qkv[...], wp[at, :]) + nn(br, d_cat[:, at])
         send(s)
         return carry
 
@@ -688,7 +685,7 @@
         scratch_shapes=[pltpu.VMEM(a.shape, a.dtype) for a in args]
         + [pltpu.VMEM((8, RANK, w), F32) for w in widths]
         + [pltpu.SemaphoreType.DMA((8,)), pltpu.SemaphoreType.DMA((14,))],
-        compiler_params=pltpu.CompilerParams(vmem_limit_bytes=40 * 1024 * 1024),
+        compiler_params=pltpu.CompilerParams(vmem_limit_bytes=60 * 1024 * 1024),
     )(*args)
 
 
@@ -714,7 +711,7 @@
         scratch_shapes=[
             pltpu.VMEM((s, n, d), BF16),
             pltpu.VMEM((s, n, d), BF16),
-            pltpu.VMEM((3, d, hw), BF16),
+            pltpu.VMEM((d, 3 * hw), BF16),
             pltpu.VMEM((hw, d), BF16),
             pltpu.VMEM((d, f), BF16),
             pltpu.VMEM((f, d), BF16),
@@ -731,9 +728,13 @@
             pltpu.VMEM((s, n, d), F32),
             pltpu.VMEM((s, n, d), F32),
             pltpu.VMEM((n, d), BF16),
-            pltpu.VMEM((5, n, hw), BF16),
+            pltpu.VMEM((n, hw), BF16),
+            pltpu.VMEM((n, 3 * hw), BF16),
+            pltpu.VMEM((hw, n), BF16),
+            pltpu.VMEM((128, 3 * hw), BF16),
+            pltpu.VMEM((128, d), BF16),
             pltpu.VMEM((n, 128), F32),
-            pltpu.VMEM((s, 3, RANK, n), BF16),
+            pltpu.VMEM((s, 3 * RANK, n), BF16),
             pltpu.VMEM((s, RANK, n), BF16),
             pltpu.VMEM((RANK, n), F32),
             pltpu.VMEM((s, 6 * RANK, n), F32),

time: 183 us -> 158 us (0.86)
  Pallas kernels: 170 us -> 156 us
  local copies, waits for them, and re-layouts: 10.5 us -> 0 us
    pallas_call x1, Pallas kernels: 165 us -> 148 us  [layer(): pl.pallas_call(layer_kernel, out_shape=(sds((s, n, d), BF16), sds((s, n,...]
    unnamed x16 -> x0, local copies, waits for them, and re-layouts: 10.5 us -> none
    pallas_call x1, Pallas kernels: 4.92 us -> 7.81 us  [place(): pl.pallas_call(place_kernel, out_shape=[jax.ShapeDtypeStruct((s, n, d), B...]
where the time goes in v3:
time: 158 us
  Pallas kernels  156 us (99%)
    pallas_call x1, Pallas kernels, layer(): pl.pallas_call(layer_kernel, out_shape=(sds((s, n, d), BF16), sds((s, n,...  148 us
    pallas_call x1, Pallas kernels, place(): pl.pallas_call(place_kernel, out_shape=[jax.ShapeDtypeStruct((s, n, d), B...  7.81 us

profile of v3, /device:TPU:0, one launch (start us, length us, event | category | flops | bytes accessed | tf_op | source)
XLA Modules:
  0.0 157.6 jit_solution(10445566671380733346)
XLA Ops:
  0.6 1.3 convert_element_type.3.seg
  1.9 147.7 %shard_map.353 = (bf16[2,512,1024]{2,1,0:T(8,128)(2,1)}, bf16[2,512,1024]{2,1,0:T(8,128)(2,1)}, f32[16,8,8,512]{3,2,1,0:T(8,128)}, f32[16,8,8,128]{3,2,1,0:T(8,1...) custom-call(s32[2]{0:T(128)} %ids.1, ...), custom_call_target="tpu_custom_call" | custom-call | tf_op jit(solution)/shard_map/pallas_call | solution.py:700
  149.7 7.8 %shard_map.354 = (bf16[2,512,1024]{2,1,0:T(8,128)(2,1)}, bf16[2,512,1024]{2,1,0:T(8,128)(2,1)}, f32[8,16,1024]{2,1,0:T(8,128)}, f32[8,16,512]{2,1,0:T(8,128)}, f...) custom-call(f32[16,8,8,512]{3,2,1,0:T(8,128)} %get-tuple-element.36., ...), custom_call_target="tpu_custom_call" | custom-call | tf_op jit(solution)/shard_map/pallas_call | solution.py:679

commit v4 on v3

--- a/solution.py
+++ b/solution.py
@@ -13,7 +13,9 @@
 EPS = 1e-05
 ROWS = 128
 GROUP = 16
-EARLY, LATE = 640, 512
+LANES = (256, 384, 128, 384)
+GROUPS = range(len(LANES))
+SWAPPED = (1, 2, 3)
 
 
 def nn(a, b):
@@ -47,11 +49,11 @@
 
 def layer_kernel(
     ids, seg, x_hbm, cot_hbm, wq, wk, wv, wo_hbm, we_hbm, wc_hbm, g1, b1, g2, b2,
-    qd, kd, vd, qu, ku, vu, od, ou, ed, eu, cd, cu,
-    out_hbm, grad_hbm, geu, ger, glu, glr, her, hlr,
+    qd, kd, vd, qu, ku, vu, od_hbm, ou_hbm, ed_hbm, eu_hbm, cd_hbm, cu_hbm,
+    out_hbm, grad_hbm, g0, g1_, g2_, g3, h1, h2, h3,
     x, cot, wp, wo, we, wc, dtab, utab, qkv, heads, bias, lse, xhat, rstd, hidden, slope, acc, recv,
-    row, d_heads, d_qkv, dq_t, u_cat, d_cat, lcol, rank_t, rank_e, drow, mine_rk, their_rk, stage_out,
-    pick_mine, picks, pack_e, pack_l, rs_e, rs_l, dense_eu, dense_er, dense_lu, dense_lr,
+    od, ou, ed, eu, cd, cu, row, back_rank, u_cat, d_cat, lcol, rank_t, rank_e, drow, mine_rk, their_rk, stage_out,
+    pick_mine, picks, p0, p1, p2, p3, r0, r1, r2, r3, d0, d1, d2, d3,
     load_sem, send_sem, recv_sem, out_sem, credit, rk_send, rk_recv, pick_send, pick_recv,
     rs_send_sem, rs_recv_sem, z_send, z_recv, plane_send, plane_recv, own_sem, swap_send, swap_recv,
 ):
@@ -64,20 +66,20 @@
     half = pl.ds(pl.multiple_of(core * 512, 512), 512)
 
     def load(i, src, dst):
-        cp = pltpu.make_async_copy(src, dst, load_sem.at[i])
+        return pltpu.make_async_copy(src, dst, load_sem.at[i])
+
+    load_x = [load(s, x_hbm.at[s], x.at[s]) for s in range(2)]
+    load_d = [load(2 + i, t, dtab.at[i]) for i, t in enumerate((qd, kd, vd))]
+    load_u = [load(5 + i, t, utab.at[i]) for i, t in enumerate((qu, ku, vu))]
+    load_w = [load(8 + i, t, wp.at[:, pl.ds(512 * i, 512)]) for i, t in enumerate((wq, wk, wv))]
+    load_o = [load(11, wo_hbm, wo), load(12, od_hbm, od), load(13, ou_hbm, ou)]
+    load_f = [
+        load(14, we_hbm, we), load(15, ed_hbm, ed), load(16, eu_hbm, eu),
+        load(17, wc_hbm, wc), load(18, cd_hbm, cd), load(19, cu_hbm, cu),
+    ]
+    load_cot = load(20, cot_hbm, cot)
+    for cp in load_x[:1] + load_d + load_w + load_u:
         cp.start()
-        return cp
-
-    loads = [load(0, x_hbm, x)]
-    tabs = []
-    for i, (w, d, u) in enumerate(((wq, qd, qu), (wk, kd, ku), (wv, vd, vu))):
-        tabs.append(load(1 + i, w, wp.at[:, pl.ds(512 * i, 512)]))
-        tabs.append(load(4 + i, d, dtab.at[i]))
-        tabs.append(load(7 + i, u, utab.at[i]))
-    load_wo = load(10, wo_hbm, wo)
-    load_we = load(11, we_hbm, we)
-    load_wc = load(12, wc_hbm, wc)
-    load_cot = load(13, cot_hbm, cot)
 
     def peer(k):
         return (base + lax.bitwise_xor(me, k), core)
@@ -90,7 +92,6 @@
         return c
 
     lax.fori_loop(1, GROUP, greet, 0)
-    pl.semaphore_wait(barrier, GROUP)
 
     def remote(src, dst, ss, rs, to):
         return pltpu.make_async_remote_copy(
@@ -109,7 +110,9 @@
         pick_copy(k).start()
         return c
 
-    lax.fori_loop(1, GROUP, send_pick, 0)
+    def meet():
+        pl.semaphore_wait(barrier, GROUP)
+        lax.fori_loop(1, GROUP, send_pick, 0)
 
     def rk_copy(s, i):
         rows = pl.ds(i * RANK, RANK if i < 3 else 3 * RANK)
@@ -122,8 +125,14 @@
         at = slice(i * RANK, i * RANK + rows)
         return mine_rk[s, at, :] + their_rk[s, at, :]
 
-    packs, parts, swapped = (pack_e, pack_l), (rs_e, rs_l), (her, hlr)
-    denses, gathered = ((dense_eu, dense_er), (dense_lu, dense_lr)), ((geu, ger), (glu, glr))
+    packs, parts, denses = (p0, p1, p2, p3), (r0, r1, r2, r3), (d0, d1, d2, d3)
+    gathered, swapped = (g0, g1_, g2_, g3), (None, h1, h2, h3)
+
+    def pack(g, s, col, v):
+        for b in range(v.shape[1] // 128):
+            cut, ln = divmod(col + 128 * b, LANES[g])
+            for h in range(2):
+                packs[g][s, 2 * cut + h, :, ln:ln + 128] = v[8 * h:8 * h + 8, 128 * b:128 * b + 128]
 
     def shard_copy(g, s, k):
         to = lax.bitwise_xor(me, k)
@@ -148,89 +157,119 @@
 
         lax.fori_loop(1, GROUP, wait, 0)
 
+        cuts = range(0, LANES[g], 128)
+
         def add(m, total):
             for s in range(2):
-                part = parts[g][m, s]
-                total = tuple(
-                    t + part * jnp.broadcast_to(picks[m, s, a:a + 1, 0:1], part.shape)
-                    for a, t in enumerate(total)
-                )
-            return total
-
-        zero = jnp.zeros(parts[g].shape[2:], F32)
-        for a, t in enumerate(lax.fori_loop(0, GROUP, add, (zero,) * 8)):
-            w = denses[g][0].shape[2]
-            denses[g][0][a] = t[:, :w]
-            denses[g][1][a] = t[:, w:]
-
-    def own_copy(g, i):
-        return pltpu.make_async_copy(denses[g][i], gathered[g][i].at[me], own_sem.at[g, i])
-
-    def z_copy(g, i, u):
-        return remote(
-            denses[g][i], gathered[g][i].at[me], z_send.at[g, i, u], z_recv.at[g, i, u], peer(4 * u)
-        )
+                part = [parts[g][m, s, :, at:at + 128] for at in cuts]
+                for a in range(8):
+                    weight = jnp.broadcast_to(picks[m, s, a:a + 1, :], (8, 128))
+                    total = [
+                        t + weight * part[i % len(cuts)] if i // len(cuts) == a else t
+                        for i, t in enumerate(total)
+                    ]
+            return tuple(total)
+
+        total = lax.fori_loop(0, GROUP, add, (jnp.zeros((8, 128), F32),) * (8 * len(cuts)))
+        for i, t in enumerate(total):
+            a, at = divmod(i, len(cuts))
+            denses[g][a, :, 128 * at:128 * at + 128] = t
+
+    def own_copy(g):
+        return pltpu.make_async_copy(denses[g], gathered[g].at[me], own_sem.at[g])
+
+    def z_copy(g, u):
+        return remote(denses[g], gathered[g].at[me], z_send.at[g, u], z_recv.at[g, u], peer(4 * u))
 
     def slot(u, k):
         return lax.bitwise_xor(me, 4 * u + k)
 
-    def plane_copy(g, i, u, way):
-        to = gathered[g][i].at[slot(u, 0)]
+    def plane_copy(g, u, way):
+        to = gathered[g].at[slot(u, 0)]
         return remote(
-            denses[g][i] if u == 0 else to, to, plane_send.at[g, i, u, way], plane_recv.at[g, i, u, way],
-            peer(way + 1),
+            denses[g] if u == 0 else to, to, plane_send.at[g, u, way], plane_recv.at[g, u, way], peer(way + 1)
         )
 
-    def onward_copy(g, i, u, way):
-        at = gathered[g][i].at[slot(u, way + 1), pl.ds(4 * way, 4)]
-        return remote(
-            at, at, plane_send.at[g, i, u, 2 + way], plane_recv.at[g, i, u, 2 + way], peer(2 - way)
+    def onward_copy(g, u, way):
+        at = gathered[g].at[slot(u, way + 1), pl.ds(4 * way, 4)]
+        return remote(at, at, plane_send.at[g, u, 2 + way], plane_recv.at[g, u, 2 + way], peer(2 - way))
+
+    def swap_copy(g, u):
+        plane = lax.bitwise_xor(me // 4, u)
+        return plane >= 2, remote(
+            gathered[g].at[pl.ds(4 * plane, 4)], swapped[g].at[pl.ds(4 * lax.rem(plane, 2), 4)],
+            swap_send.at[g, u], swap_recv.at[g, u], partner,
         )
 
-    def swap_copy(g, u):
-        plane = pl.ds(slot(u, 0) // 4 * 4, 4)
-        return remote(
-            gathered[g][1].at[plane], swapped[g].at[plane], swap_send.at[g, u], swap_recv.at[g, u], partner
-        )
-
-    both = [(i, way) for i in range(2) for way in range(2)]
-
     def gather_first(g):
-        for i in range(2):
-            own_copy(g, i).start()
-            for u in (1, 2, 3):
-                z_copy(g, i, u).start()
-        for i, way in both:
-            plane_copy(g, i, 0, way).start()
+        own_copy(g).start()
+        for u in (1, 2, 3):
+            z_copy(g, u).start()
+        for way in range(2):
+            plane_copy(g, 0, way).start()
 
     def gather_unit(g, u):
-        for i in range(2):
-            z_copy(g, i, u).wait_recv()
-        for i, way in both:
-            plane_copy(g, i, u, way).start()
+        z_copy(g, u).wait_recv()
+        for way in range(2):
+            plane_copy(g, u, way).start()
 
     def gather_onward(g, u):
-        for i, way in both:
-            plane_copy(g, i, u, way).wait_recv()
-            onward_copy(g, i, u, way).start()
+        for way in range(2):
+            plane_copy(g, u, way).wait_recv()
+            onward_copy(g, u, way).start()
 
     def gather_swap(g, u):
         if u == 0:
-            for i in range(2):
-                own_copy(g, i).wait()
-        for i, way in both:
-            onward_copy(g, i, u, way).wait_recv()
-        swap_copy(g, u).start()
+            own_copy(g).wait()
+        for way in range(2):
+            onward_copy(g, u, way).wait_recv()
+        if g in SWAPPED:
+            upper, copy = swap_copy(g, u)
+
+            @pl.when(upper)
+            def _():
+                copy.start()
 
     def gather_end(g):
         for u in (1, 2, 3):
-            for i in range(2):
-                z_copy(g, i, u).wait_send()
+            z_copy(g, u).wait_send()
         for u in range(4):
-            for i, way in both:
-                plane_copy(g, i, u, way).wait_send()
-                onward_copy(g, i, u, way).wait_send()
-            swap_copy(g, u).wait()
+            for way in range(2):
+                plane_copy(g, u, way).wait_send()
+                onward_copy(g, u, way).wait_send()
+            if g in SWAPPED:
+                upper, copy = swap_copy(g, u)
+
+                @pl.when(upper)
+                def _():
+                    copy.wait()
+
+    def gather_begin(g):
+        combine(g)
+        gather_first(g)
+
+    def gather_step(g, u):
+        if u < 4:
+            gather_unit(g, u)
+        gather_onward(g, u - 1)
+
+    def gather_middle(g):
+        for u in (1, 2, 3):
+            gather_unit(g, u)
+        gather_onward(g, 0)
+
+    def gather_late(g):
+        for u in (1, 2, 3):
+            gather_onward(g, u)
+
+    def gather_close(g):
+        for u in range(4):
+            gather_swap(g, u)
+
+    def hosted(here, there, f):
+        @pl.when(here == there)
+        def _():
+            f()
 
     def exchange(s):
         return pltpu.make_async_remote_copy(
@@ -252,9 +291,6 @@
     lane = lax.broadcasted_iota(jnp.int32, (n, 128), 1)
     low_half = lane < HEAD_WIDTH
 
-    for cp in loads + tabs:
-        cp.wait()
-
     u_cat[...] = jnp.zeros_like(u_cat)
     d_cat[...] = jnp.zeros_like(d_cat)
 
@@ -280,15 +316,34 @@
 
     def stage1(s, carry):
         aid = ids[s]
-        seg_row = seg[pl.ds(s, 1), :]
+        seg_row = seg[pl.ds(s, 1), :].astype(F32)
         seg_col = jnp.broadcast_to(seg_row, (128, n)).T
         for j in range(n // 128):
             same = seg_col == seg_row[:, j * 128:(j + 1) * 128]
             bias[s, :, j * 128:(j + 1) * 128] = jnp.where(same, 0.0, -1e30)
+
+        @pl.when(s == 0)
+        def _():
+            for cp in load_x[:1] + load_d + load_u:
+                cp.wait()
+            for cp in load_x[1:] + load_o:
+                cp.start()
+
+        @pl.when(s == 1)
+        def _():
+            load_x[1].wait()
+
         stack_tables(aid)
         rank = jnp.where(lane < 64, nt(x[s], d_cat[...]), 0.0)
         rank_t[s] = rank.T[0:3 * RANK, :].astype(BF16)
         rank = rank.astype(BF16)
+
+        @pl.when(s == 0)
+        def _():
+            for cp in load_w:
+                cp.wait()
+            for cp in load_f + [load_cot]:
+                cp.start()
 
         def project(p, c):
             at = pl.ds(pl.multiple_of(p * hw, hw), hw)
@@ -325,7 +380,9 @@
 
         @pl.when(s == 0)
         def _():
-            load_wo.wait()
+            for cp in load_o:
+                cp.wait()
+            meet()
 
         hs = heads[s]
         ro = nt(hs, twice(od[aid]))
@@ -382,8 +439,8 @@
         send(s)
         return carry
 
-    load_we.wait()
-    load_wc.wait()
+    for cp in load_f:
+        cp.wait()
     lax.fori_loop(0, 2, stage2, 0)
 
     def put_out(s):
@@ -391,6 +448,11 @@
 
     def put_grad(s):
         return pltpu.make_async_copy(stage_out.at[s], grad_hbm.at[s], out_sem.at[s])
+
+    def early(s):
+        inner = (xhat[s, :, half] * g1[:, half] + b1[:, half]).astype(BF16)
+        pack(1, s, 2048, term(rank_sum(s, 2, RANK), inner))
+        scatter(1, s)
 
     def stage3(s, carry):
         aid = ids[s]
@@ -419,16 +481,11 @@
         brc = nt(row[...], cu[aid])
         brc_t = brc.T.astype(BF16)
         brc = brc.astype(BF16)
-        t_cu = term(rank_sum(s, 1, RANK), row[:, half])
-        for q in range(4):
-            for h in range(2):
-                pack_e[s, 8 + 2 * q + h, :, 512:640] = t_cu[8 * h:8 * h + 8, 128 * q:128 * q + 128]
+        for c in range(chunks):
+            pack(0, s, 512 * c, nn(brc_t, hidden[s, :, 512 * c:512 * c + 512]))
+        scatter(0, s)
+        pack(1, s, 2560, term(rank_sum(s, 1, RANK), row[:, half]))
         re_t = rank_e[s]
-
-        def early_parts(c, t, lanes):
-            for q in range(2):
-                for h in range(2):
-                    pack_e[s, 4 * c + 2 * q + h, :, lanes] = t[8 * h:8 * h + 8, 256 * q:256 * q + 256]
 
         def contract_back(c):
             at = slice(512 * c, 512 * c + 512)
@@ -438,11 +495,12 @@
         for c in range(chunks):
             after = contract_back(c + 1) if c + 1 < chunks else None
             at = slice(512 * c, 512 * c + 512)
-            early_parts(c, nn(brc_t, hidden[s, :, at]), slice(256, 512))
             bb = (bh * slope[s, :, at].astype(F32)).astype(BF16)
             slope[s, :, at] = bb
-            early_parts(c, nn(re_t, bb), slice(0, 256))
+            pack(1, s, 512 * c, nn(re_t, bb))
             bh = after
+            if c == 0:
+                hosted(s, 1, lambda: early(0))
         br = nt(slope[s], twice(eu[aid]))
         mine_rk[s, 2 * RANK:3 * RANK, :] = br.T[0:RANK, :]
         rk_copy(s, 2).start()
@@ -454,55 +512,27 @@
         send(s)
         return carry
 
-    load_cot.wait()
-    lax.fori_loop(0, 2, stage3, 0)
-
-    def early(s, carry):
-        inner = (xhat[s, :, half] * g1[:, half] + b1[:, half]).astype(BF16)
-        t_ed = term(rank_sum(s, 2, RANK), inner)
-        for q in range(4):
-            for h in range(2):
-                pack_e[s, 2 * q + h, :, 512:640] = t_ed[8 * h:8 * h + 8, 128 * q:128 * q + 128]
-        scatter(0, s)
-        return carry
-
-    lax.fori_loop(0, 2, early, 0)
-
-    def put_late(s, t, up, down):
-        for q in range(2):
-            for h in range(2):
-                part = slice(8 * h, 8 * h + 8), slice(256 * q, 256 * q + 256)
-                if up is not None:
-                    pack_l[s, 4 * t + 2 * q + h, :, 0:256] = up[part]
-                if down is not None:
-                    pack_l[s, 4 * t + 2 * q + h, :, 256:512] = down[part]
-
-    def between(s, hp):
-        def at(s_, hp_, f):
-            @pl.when(jnp.logical_and(s == s_, hp == hp_))
-            def _():
-                f()
-
-        def begin():
-            combine(0)
-            gather_first(0)
-
-        def step(u):
-            def f():
-                gather_unit(0, u)
-                gather_onward(0, u - 1)
-            return f
-
-        at(0, 3, begin)
-        at(1, 0, step(1))
-        at(1, 1, step(2))
-        at(1, 3, step(3))
-
     def wait_picks(k, c):
         pick_copy(k).wait()
         return c
 
     lax.fori_loop(1, GROUP, wait_picks, 0)
+
+    load_cot.wait()
+    lax.fori_loop(0, 2, stage3, 0)
+
+    early(1)
+
+    plan = {
+        (0, 0): lambda: gather_begin(0), (0, 2): lambda: gather_begin(1), (0, 3): lambda: gather_middle(0),
+        (1, 0): lambda: gather_middle(1), (1, 1): lambda: gather_late(0),
+        (1, 2): lambda: gather_begin(2), (1, 3): lambda: gather_late(1),
+    }
+
+    def between(s, hp):
+        for (s_, hp_), f in plan.items():
+            hosted(4 * s + hp, 4 * s_ + hp_, f)
+
 
     def stage4(s, carry):
         aid = ids[s]
@@ -523,15 +553,15 @@
         taken(s)
         hs = heads[s]
         bro = nt(row[...], ou[aid])
-        put_late(
-            s, 3, nn(bro.T.astype(BF16), hs), term(rank_sum(s, 0, RANK), row[:, half])
-        )
-        d_heads[...] = (nt(row[...], wo[...]) + nn(bro.astype(BF16), od[aid])).astype(BF16)
+        pack(2, s, 0, nn(bro.T.astype(BF16), hs))
+        pack(2, s, 512, term(rank_sum(s, 0, RANK), row[:, half]))
+        scatter(2, s)
+        hidden[s, :, 3 * hw:] = (nt(row[...], wo[...]) + nn(bro.astype(BF16), od[aid])).astype(BF16)
         pick = (
             lax.broadcasted_iota(jnp.int32, (RANK, hw), 1) // HEAD_WIDTH
             == lax.broadcasted_iota(jnp.int32, (RANK, hw), 0)
         ).astype(BF16)
-        hi, lo = split(d_heads[...].astype(F32) * hs.astype(F32))
+        hi, lo = split(hidden[s, :, 3 * hw:].astype(F32) * hs.astype(F32))
         drow[...] = nt(pick, hi) + nt(pick, lo)
 
         def pair(hp, c):
@@ -539,7 +569,7 @@
             q2 = qkv[s, 0, :, at]
             k2 = qkv[s, 1, :, at]
             v2 = qkv[s, 2, :, at]
-            do2 = d_heads[:, at]
+            do2 = hidden[s, :, pl.ds(pl.multiple_of(3 * hw + hp * 128, 128), 128)]
             k2t = k2.T
             zero = jnp.zeros_like(k2)
             dk, dv = [], []
@@ -553,39 +583,44 @@
                 dv.append(nn(pt.astype(BF16), do2))
                 dk.append(nn(dst, q2))
                 dqt = nn(k2t[j * HEAD_WIDTH:(j + 1) * HEAD_WIDTH, :], dst) * 0.125
-                dq_t[pl.ds(pl.multiple_of(h * HEAD_WIDTH, HEAD_WIDTH), HEAD_WIDTH), :] = dqt.astype(BF16)
+                slope[s, pl.ds(pl.multiple_of(h * HEAD_WIDTH, HEAD_WIDTH), HEAD_WIDTH), 0:n] = dqt.astype(BF16)
             to = pl.multiple_of(hp * 128, 128)
-            d_qkv[:, pl.ds(hw + to, 128)] = jnp.where(low_half, dk[0], dk[1]).astype(BF16)
-            d_qkv[:, pl.ds(2 * hw + to, 128)] = jnp.where(low_half, dv[0], dv[1]).astype(BF16)
+            hidden[s, :, pl.ds(hw + to, 128)] = jnp.where(low_half, dk[0], dk[1]).astype(BF16)
+            hidden[s, :, pl.ds(2 * hw + to, 128)] = jnp.where(low_half, dv[0], dv[1]).astype(BF16)
             between(s, hp)
             return c
 
         lax.fori_loop(0, pairs, pair, 0)
-        d_qkv[:, 0:hw] = dq_t[...].T
+        hidden[s, :, 0:hw] = slope[s, 0:hw, 0:n].T
         stack_tables(aid)
-        br = nt(d_qkv[...], u_cat[...])
+        br = nt(hidden[s, :, 0:3 * hw], u_cat[...])
         mine_rk[s, 3 * RANK:6 * RANK, :] = br.T[0:3 * RANK, :]
         rk_copy(s, 3).start()
-        br = wide(br, 64)
+        back_rank[s] = wide(br, 64)
         for p in range(3):
-            put_late(
-                s, p, nn(rank_t[s, RANK * p:RANK * p + RANK, :], d_qkv[:, hw * p:hw * p + hw]), None
+            pack(
+                3, s, 512 * p, nn(rank_t[s, RANK * p:RANK * p + RANK, :], hidden[s, :, hw * p:hw * p + hw])
             )
         t_d = term(rank_sum(s, 3, 3 * RANK), x[s, :, half])
         for p in range(3):
-            put_late(s, p, None, t_d[RANK * p:RANK * p + RANK, :])
-        scatter(1, s)
+            pack(3, s, 1536 + 512 * p, t_d[RANK * p:RANK * p + RANK, :])
+        scatter(3, s)
+        return carry
+
+    lax.fori_loop(0, 2, stage4, 0)
+
+    def project_back(s, carry):
+        stack_tables(ids[s])
         for c in range(2):
             at = slice(512 * c, 512 * c + 512)
-            acc[s, :, at] += nt(d_qkv[...], wp[at, :]) + nn(br, d_cat[:, at])
+            acc[s, :, at] += nt(hidden[s, :, 0:3 * hw], wp[at, :]) + nn(back_rank[s], d_cat[:, at])
         send(s)
         return carry
 
-    lax.fori_loop(0, 2, stage4, 0)
-
-    gather_onward(0, 3)
-
-    def stage5(s, carry):
+    lax.fori_loop(0, 2, project_back, 0)
+    gather_middle(2)
+
+    def stage5(s):
         exchange(s).wait()
         put_out(s).wait()
 
@@ -596,28 +631,30 @@
 
         lax.fori_loop(0, n // ROWS, add, 0)
         put_grad(s).start()
-        return carry
-
-    lax.fori_loop(0, 2, stage5, 0)
-    for u in range(4):
-        gather_swap(0, u)
-    combine(1)
-    gather_first(1)
-    for u in (1, 2, 3):
-        gather_unit(1, u)
-        gather_onward(1, u - 1)
-    gather_onward(1, 3)
-    for u in range(4):
-        gather_swap(1, u)
-    gather_end(0)
-    gather_end(1)
+
+    gather_begin(3)
+    gather_late(2)
+    stage5(0)
+    gather_step(3, 1)
+    stage5(1)
+    for g in (0, 1, 2):
+        gather_close(g)
+    gather_step(3, 2)
+    gather_swap(3, 0)
+    gather_step(3, 3)
+    gather_swap(3, 1)
+    gather_step(3, 4)
+    gather_swap(3, 2)
+    gather_swap(3, 3)
+    for g in GROUPS:
+        gather_end(g)
     put_grad(0).wait()
     put_grad(1).wait()
 
 
 def place_kernel(*refs):
-    src, dst, src_v, dst_v = refs[:8], refs[8:22], refs[22:30], refs[30:42]
-    in_sem, out_sem = refs[42:]
+    src, dst, src_v, dst_v = refs[:9], refs[9:23], refs[23:32], refs[32:44]
+    in_sem, out_sem = refs[44:]
     core = lax.axis_index("tensor")
     loads = [pltpu.make_async_copy(a, b, in_sem.at[i]) for i, (a, b) in enumerate(zip(src, src_v))]
     for cp in loads:
@@ -630,43 +667,44 @@
         ends.append(cp)
 
     qd, qu, kd, ku, vd, vu, od, ou, ed, eu, cd, cu = range(12)
-    up, down, low = (qu, ku, vu, od), (qd, kd, vd, ou), (ed, cu)
-    geu, ger, glu, glr, her, hlr = src_v[:6]
-
-    def lanes(side, width, i):
-        return pl.ds(pl.multiple_of(side * 512 + width * i, 128), width)
-
-    def rows(n):
-        return slice(8 * (n % 2), 8 * (n % 2) + 8)
+    swapped = (None,) + tuple(src_v[4:7])
+
+    def lanes(side, b):
+        return pl.ds(pl.multiple_of(side * 512 + 128 * b, 128), 128)
+
+    def fill(g, col, table, count, split_table):
+        for b in range(count):
+            cut, ln = divmod(col + 128 * b, LANES[g])
+            for h in range(2):
+                rows = slice(8 * h, 8 * h + 8)
+                n, ls = 2 * cut + h, slice(ln, ln + 128)
+                v = src_v[g][n, :, :, ls]
+                if split_table:
+                    dst_v[table][:, rows, lanes(core, b)] = v
+                    dst_v[table][:, rows, lanes(1 - core, b)] = swapped[g][n - 8, :, :, ls]
+                else:
+                    dst_v[table][:, rows, 128 * b:128 * b + 128] = v
+        store(dst_v[table], 2 + table)
 
     loads[0].wait()
-    for n in range(GROUP):
-        at = slice(256 * (n // 2), 256 * (n // 2) + 256)
-        dst_v[eu][:, rows(n), at] = geu[n, :, :, 0:256]
-        dst_v[cd][:, rows(n), at] = geu[n, :, :, 256:512]
-    store(dst_v[eu], 2 + eu)
-    store(dst_v[cd], 2 + cd)
+    fill(0, 0, cd, 16, False)
     for i in (1, 4):
         loads[i].wait()
-    for n in range(GROUP):
-        v = dst_v[low[n // 8]]
-        v[:, rows(n), lanes(core, 128, n % 8 // 2)] = ger[n]
-        v[:, rows(n), lanes(1 - core, 128, n % 8 // 2)] = her[n]
-    store(dst_v[ed], 2 + ed)
-    store(dst_v[cu], 2 + cu)
-    for i in (2, 3, 5):
+    fill(1, 0, eu, 16, False)
+    fill(1, 2048, ed, 4, True)
+    fill(1, 2560, cu, 4, True)
+    for i in (2, 5):
         loads[i].wait()
-    for t in range(4):
-        for n in range(4 * t, 4 * t + 4):
-            q = n % 4 // 2
-            dst_v[up[t]][:, rows(n), 256 * q:256 * q + 256] = glu[n]
-            dst_v[down[t]][:, rows(n), lanes(core, 256, q)] = glr[n]
-            dst_v[down[t]][:, rows(n), lanes(1 - core, 256, q)] = hlr[n]
-        store(dst_v[up[t]], 2 + up[t])
-        store(dst_v[down[t]], 2 + down[t])
+    fill(2, 0, od, 4, False)
+    fill(2, 512, ou, 4, True)
+    for i in (3, 6):
+        loads[i].wait()
+    for p, (up, down) in enumerate(((qu, qd), (ku, kd), (vu, vd))):
+        fill(3, 512 * p, up, 4, False)
+        fill(3, 1536 + 512 * p, down, 4, True)
     for i in range(2):
-        loads[6 + i].wait()
-        store(src_v[6 + i], i)
+        loads[7 + i].wait()
+        store(src_v[7 + i], i)
     for cp in ends:
         cp.wait()
 
@@ -680,11 +718,11 @@
         place_kernel,
         out_shape=[jax.ShapeDtypeStruct((s, n, d), BF16)] * 2
         + [jax.ShapeDtypeStruct((8, RANK, w), F32) for w in widths],
-        in_specs=[hbm] * 8,
+        in_specs=[hbm] * 9,
         out_specs=[hbm] * 14,
         scratch_shapes=[pltpu.VMEM(a.shape, a.dtype) for a in args]
         + [pltpu.VMEM((8, RANK, w), F32) for w in widths]
-        + [pltpu.SemaphoreType.DMA((8,)), pltpu.SemaphoreType.DMA((14,))],
+        + [pltpu.SemaphoreType.DMA((9,)), pltpu.SemaphoreType.DMA((14,))],
         compiler_params=pltpu.CompilerParams(vmem_limit_bytes=60 * 1024 * 1024),
     )(*args)
 
@@ -701,13 +739,12 @@
         layer_kernel,
         out_shape=(
             sds((s, n, d), BF16), sds((s, n, d), BF16),
-            sds((GROUP, 8, 8, 512), F32), sds((GROUP, 8, 8, 128), F32),
-            sds((GROUP, 8, 8, 256), F32), sds((GROUP, 8, 8, 256), F32),
-            sds((GROUP, 8, 8, 128), F32), sds((GROUP, 8, 8, 256), F32),
+            *(sds((GROUP, 8, 8, w), F32) for w in LANES),
+            *(sds((GROUP // 2, 8, 8, LANES[g]), F32) for g in SWAPPED),
         ),
         in_specs=[sm, vm, hbm, hbm, hbm, hbm, hbm, hbm, hbm, hbm, vm, vm, vm, vm]
-        + [hbm] * 6 + [vm] * 6,
-        out_specs=(hbm,) * 8,
+        + [hbm] * 12,
+        out_specs=(hbm,) * 9,
         scratch_shapes=[
             pltpu.VMEM((s, n, d), BF16),
             pltpu.VMEM((s, n, d), BF16),
@@ -727,10 +764,9 @@
             pltpu.VMEM((s, n, f), BF16),
             pltpu.VMEM((s, n, d), F32),
             pltpu.VMEM((s, n, d), F32),
+            *(pltpu.VMEM((8, RANK, w), BF16) for w in (hw, d, d, f, f, d)),
             pltpu.VMEM((n, d), BF16),
-            pltpu.VMEM((n, hw), BF16),
-            pltpu.VMEM((n, 3 * hw), BF16),
-            pltpu.VMEM((hw, n), BF16),
+            pltpu.VMEM((s, n, 128), BF16),
             pltpu.VMEM((128, 3 * hw), BF16),
             pltpu.VMEM((128, d), BF16),
             pltpu.VMEM((n, 128), F32),
@@ -742,15 +778,10 @@
             pltpu.VMEM((s, n, d), BF16),
             pltpu.VMEM((s, 8, 128), F32),
             pltpu.VMEM((GROUP, s, 8, 128), F32),
-            pltpu.VMEM((s, GROUP, 8, EARLY), F32),
-            pltpu.VMEM((s, GROUP, 8, LATE), F32),
-            pltpu.VMEM((GROUP, s, 8, EARLY), F32),
-            pltpu.VMEM((GROUP, s, 8, LATE), F32),
-            pltpu.VMEM((8, 8, 512), F32),
-            pltpu.VMEM((8, 8, 128), F32),
-            pltpu.VMEM((8, 8, 256), F32),
-            pltpu.VMEM((8, 8, 256), F32),
-            pltpu.SemaphoreType.DMA((14,)),
+            *(pltpu.VMEM((s, GROUP, 8, w), F32) for w in LANES),
+            *(pltpu.VMEM((GROUP, s, 8, w), F32) for w in LANES),
+            *(pltpu.VMEM((8, 8, w), F32) for w in LANES),
+            pltpu.SemaphoreType.DMA((21,)),
             pltpu.SemaphoreType.DMA((2,)),
             pltpu.SemaphoreType.DMA((2,)),
             pltpu.SemaphoreType.DMA((2,)),
@@ -759,15 +790,11 @@
             pltpu.SemaphoreType.DMA((2, 4)),
             pltpu.SemaphoreType.DMA((GROUP,)),
             pltpu.SemaphoreType.DMA((GROUP,)),
-            pltpu.SemaphoreType.DMA((2, 2, GROUP)),
-            pltpu.SemaphoreType.DMA((2, 2, GROUP)),
-            pltpu.SemaphoreType.DMA((2, 2, 4)),
-            pltpu.SemaphoreType.DMA((2, 2, 4)),
-            pltpu.SemaphoreType.DMA((2, 2, 4, 4)),
-            pltpu.SemaphoreType.DMA((2, 2, 4, 4)),
-            pltpu.SemaphoreType.DMA((2, 2)),
-            pltpu.SemaphoreType.DMA((2, 4)),
-            pltpu.SemaphoreType.DMA((2, 4)),
+            *(pltpu.SemaphoreType.DMA((len(LANES), 2, GROUP)),) * 2,
+            *(pltpu.SemaphoreType.DMA((len(LANES), 4)),) * 2,
+            *(pltpu.SemaphoreType.DMA((len(LANES), 4, 4)),) * 2,
+            pltpu.SemaphoreType.DMA((len(LANES),)),
+            *(pltpu.SemaphoreType.DMA((len(LANES), 4)),) * 2,
         ],
         compiler_params=pltpu.CompilerParams(
             collective_id=0, has_side_effects=True, vmem_limit_bytes=63 * 1024 * 1024
@@ -786,7 +813,7 @@
     turn = lambda t: jnp.swapaxes(t, 1, 2)
     line = lambda v: v.reshape(1, -1)
     out, grad, *tables = layer(
-        adapter_ids, segment_ids.astype(F32),
+        adapter_ids, segment_ids,
         tokens.reshape(seqs, length, width), cotangent.reshape(seqs, length, width),
         query_weight, key_weight, value_weight, output_weight, expand_weight, contract_weight,
         line(first_gain), line(first_shift), line(second_gain), line(second_shift),

time: 158 us -> 142 us (0.90)
  Pallas kernels: 156 us -> 141 us
    pallas_call x1, Pallas kernels: 148 us -> 134 us  [layer(): pl.pallas_call(layer_kernel, out_shape=(sds((s, n, d), BF16), sds((s, n,...]
where the time goes in v4:
time: 142 us
  Pallas kernels  141 us (99%)
    pallas_call x1, Pallas kernels, layer(): pl.pallas_call(layer_kernel, out_shape=(sds((s, n, d), BF16), sds((s, n,...  134 us
    pallas_call x1, Pallas kernels, place(): pl.pallas_call(place_kernel, out_shape=[jax.ShapeDtypeStruct((s, n, d), B...  7.19 us

profile of v4, /device:TPU:0, one launch (start us, length us, event | category | flops | bytes accessed | tf_op | source)
XLA Modules:
  0.0 141.9 jit_solution(6792703656983726279)
XLA Ops:
  0.7 133.9 %shard_map.353 = (bf16[2,512,1024]{2,1,0:T(8,128)(2,1)}, bf16[2,512,1024]{2,1,0:T(8,128)(2,1)}, f32[16,8,8,256]{3,2,1,0:T(8,128)}, f32[16,8,8,384]{3,2,1,0:T(8,1...) custom-call(s32[2]{0:T(128)} %ids.1, ...), custom_call_target="tpu_custom_call" | custom-call | tf_op jit(solution)/shard_map/pallas_call | solution.py:738
  134.6 7.2 %shard_map.354 = (bf16[2,512,1024]{2,1,0:T(8,128)(2,1)}, bf16[2,512,1024]{2,1,0:T(8,128)(2,1)}, f32[8,16,1024]{2,1,0:T(8,128)}, f32[8,16,512]{2,1,0:T(8,128)}, f...) custom-call(f32[16,8,8,256]{3,2,1,0:T(8,128)} %get-tuple-element.37., ...), custom_call_target="tpu_custom_call" | custom-call | tf_op jit(solution)/shard_map/pallas_call | solution.py:717

commit v5 on v4

--- a/solution.py
+++ b/solution.py
@@ -13,8 +13,9 @@
 EPS = 1e-05
 ROWS = 128
 GROUP = 16
-LANES = (256, 384, 128, 384)
+LANES = (256, 384, 256, 256)
 GROUPS = range(len(LANES))
+RK = (0, 16, 32, 48, 80, 96)
 SWAPPED = (1, 2, 3)
 
 
@@ -37,9 +38,8 @@
 
 
 def gelu_parts(v):
-    z = jnp.abs(v) * 0.7071067811865476
-    t = 1.0 / (1.0 + 0.3275911 * z)
-    e = jnp.exp(v * v * -0.5)
+    t = 1.0 / (1.0 + 0.23164188 * jnp.abs(v))
+    e = jnp.exp2(v * v * -0.7213475204444817)
     tail = t * (
         0.127414796 + t * (-0.142248368 + t * (0.7107068705 + t * (-0.7265760135 + t * 0.5307027145)))
     ) * e
@@ -51,7 +51,7 @@
     ids, seg, x_hbm, cot_hbm, wq, wk, wv, wo_hbm, we_hbm, wc_hbm, g1, b1, g2, b2,
     qd, kd, vd, qu, ku, vu, od_hbm, ou_hbm, ed_hbm, eu_hbm, cd_hbm, cu_hbm,
     out_hbm, grad_hbm, g0, g1_, g2_, g3, h1, h2, h3,
-    x, cot, wp, wo, we, wc, dtab, utab, qkv, heads, bias, lse, xhat, rstd, hidden, slope, acc, recv,
+    x, cot, wp, wo, ff, dtab, utab, qkv, heads, bias, lse, xhat, rstd, hidden, slope, acc, recv,
     od, ou, ed, eu, cd, cu, row, back_rank, u_cat, d_cat, lcol, rank_t, rank_e, drow, mine_rk, their_rk, stage_out,
     pick_mine, picks, p0, p1, p2, p3, r0, r1, r2, r3, d0, d1, d2, d3,
     load_sem, send_sem, recv_sem, out_sem, credit, rk_send, rk_recv, pick_send, pick_recv,
@@ -65,6 +65,9 @@
     base = dp - me
     half = pl.ds(pl.multiple_of(core * 512, 512), 512)
 
+    wc, we = ff.at[0], ff.at[1]
+    d = x.shape[2]
+
     def load(i, src, dst):
         return pltpu.make_async_copy(src, dst, load_sem.at[i])
 
@@ -74,10 +77,12 @@
     load_w = [load(8 + i, t, wp.at[:, pl.ds(512 * i, 512)]) for i, t in enumerate((wq, wk, wv))]
     load_o = [load(11, wo_hbm, wo), load(12, od_hbm, od), load(13, ou_hbm, ou)]
     load_f = [
-        load(14, we_hbm, we), load(15, ed_hbm, ed), load(16, eu_hbm, eu),
-        load(17, wc_hbm, wc), load(18, cd_hbm, cd), load(19, cu_hbm, cu),
+        load(14, we_hbm.at[:, pl.ds(0, d)], we.at[pl.ds(0, d)]),
+        load(15, we_hbm.at[:, pl.ds(d, d)], we.at[pl.ds(d, d)]),
+        load(16, ed_hbm, ed), load(17, eu_hbm, eu),
+        load(18, wc_hbm, wc), load(19, cd_hbm, cd), load(20, cu_hbm, cu),
     ]
-    load_cot = load(20, cot_hbm, cot)
+    load_cot = load(21, cot_hbm, cot)
     for cp in load_x[:1] + load_d + load_w + load_u:
         cp.start()
 
@@ -115,14 +120,14 @@
         lax.fori_loop(1, GROUP, send_pick, 0)
 
     def rk_copy(s, i):
-        rows = pl.ds(i * RANK, RANK if i < 3 else 3 * RANK)
+        rows = pl.ds(RK[i], RK[i + 1] - RK[i])
         return remote(
             mine_rk.at[s, rows], their_rk.at[s, rows], rk_send.at[s, i], rk_recv.at[s, i], partner
         )
 
-    def rank_sum(s, i, rows):
+    def rank_sum(s, i):
         rk_copy(s, i).wait()
-        at = slice(i * RANK, i * RANK + rows)
+        at = slice(RK[i], RK[i + 1])
         return mine_rk[s, at, :] + their_rk[s, at, :]
 
     packs, parts, denses = (p0, p1, p2, p3), (r0, r1, r2, r3), (d0, d1, d2, d3)
@@ -340,13 +345,13 @@
 
         @pl.when(s == 0)
         def _():
-            for cp in load_w:
-                cp.wait()
             for cp in load_f + [load_cot]:
                 cp.start()
 
         def project(p, c):
             at = pl.ds(pl.multiple_of(p * hw, hw), hw)
+            for i in range(3):
+                hosted(3 * s + p, i, lambda: load_w[i].wait())
             scale = jnp.where(p == 0, 0.125, 1.0)
             qkv[s, p] = ((nn(x[s], wp[:, at]) + nn(rank, u_cat[:, at])) * scale).astype(BF16)
             return c
@@ -418,7 +423,8 @@
 
         def expand(c):
             at = slice(512 * c, 512 * c + 512)
-            return nn(row[...], we[:, at]) + nn(rank, eu[aid, :, at])
+            top, left = divmod(512 * c, d)
+            return nn(row[...], we[d * top:d * top + d, left:left + 512]) + nn(rank, eu[aid, :, at])
 
         before = expand(0)
         for c in range(chunks):
@@ -451,7 +457,7 @@
 
     def early(s):
         inner = (xhat[s, :, half] * g1[:, half] + b1[:, half]).astype(BF16)
-        pack(1, s, 2048, term(rank_sum(s, 2, RANK), inner))
+        pack(1, s, 2048, term(rank_sum(s, 2), inner))
         scatter(1, s)
 
     def stage3(s, carry):
@@ -484,7 +490,7 @@
         for c in range(chunks):
             pack(0, s, 512 * c, nn(brc_t, hidden[s, :, 512 * c:512 * c + 512]))
         scatter(0, s)
-        pack(1, s, 2560, term(rank_sum(s, 1, RANK), row[:, half]))
+        pack(1, s, 2560, term(rank_sum(s, 1), row[:, half]))
         re_t = rank_e[s]
 
         def contract_back(c):
@@ -508,7 +514,10 @@
         ed2 = twice(ed[aid])
         for c in range(2):
             at = slice(512 * c, 512 * c + 512)
-            acc[s, :, at] += nt(slope[s], we[at, :]) + nn(br, ed2[:, at])
+            low = slice(d + 512 * c, d + 512 * c + 512)
+            acc[s, :, at] += (
+                nt(slope[s, :, 0:d], we[at, :]) + nt(slope[s, :, d:], we[low, :]) + nn(br, ed2[:, at])
+            )
         send(s)
         return carry
 
@@ -523,16 +532,14 @@
 
     early(1)
 
-    plan = {
-        (0, 0): lambda: gather_begin(0), (0, 2): lambda: gather_begin(1), (0, 3): lambda: gather_middle(0),
-        (1, 0): lambda: gather_middle(1), (1, 1): lambda: gather_late(0),
-        (1, 2): lambda: gather_begin(2), (1, 3): lambda: gather_late(1),
-    }
-
-    def between(s, hp):
-        for (s_, hp_), f in plan.items():
-            hosted(4 * s + hp, 4 * s_ + hp_, f)
-
+    def finish(g, s):
+        if g == 2:
+            pack(2, s, 1536, term(rank_sum(s, 4), x[s, :, half]))
+        else:
+            t_d = term(rank_sum(s, 3), x[s, :, half])
+            pack(3, s, 1024, t_d[0:RANK, :])
+            pack(3, s, 1536, t_d[RANK:2 * RANK, :])
+        scatter(g, s)
 
     def stage4(s, carry):
         aid = ids[s]
@@ -554,15 +561,50 @@
         hs = heads[s]
         bro = nt(row[...], ou[aid])
         pack(2, s, 0, nn(bro.T.astype(BF16), hs))
-        pack(2, s, 512, term(rank_sum(s, 0, RANK), row[:, half]))
-        scatter(2, s)
+        pack(2, s, 1024, term(rank_sum(s, 0), row[:, half]))
+        hosted(s, 0, lambda: gather_begin(0))
+        hosted(s, 1, lambda: finish(2, 0))
+        hosted(s, 1, lambda: gather_middle(0))
         hidden[s, :, 3 * hw:] = (nt(row[...], wo[...]) + nn(bro.astype(BF16), od[aid])).astype(BF16)
         pick = (
             lax.broadcasted_iota(jnp.int32, (RANK, hw), 1) // HEAD_WIDTH
             == lax.broadcasted_iota(jnp.int32, (RANK, hw), 0)
         ).astype(BF16)
         hi, lo = split(hidden[s, :, 3 * hw:].astype(F32) * hs.astype(F32))
-        drow[...] = nt(pick, hi) + nt(pick, lo)
+        drow[s] = nt(pick, hi) + nt(pick, lo)
+
+        def pair(hp, c):
+            at = pl.ds(pl.multiple_of(hp * 128, 128), 128)
+            q2 = qkv[s, 0, :, at]
+            k2 = qkv[s, 1, :, at]
+            do2 = hidden[s, :, pl.ds(pl.multiple_of(3 * hw + hp * 128, 128), 128)]
+            dv = []
+            for j in range(2):
+                mine = low_half if j == 0 else jnp.logical_not(low_half)
+                st = nt(jnp.where(mine, k2, jnp.zeros_like(k2)), q2) + bias[s]
+                pt = jnp.exp(st - lse[s, pl.ds(2 * hp + j, 1), :]).astype(BF16)
+                ff[s, pl.ds(pl.multiple_of(hp * n, n), n), j * n:j * n + n] = pt
+                dv.append(nn(pt, do2))
+            to = pl.ds(pl.multiple_of(2 * hw + hp * 128, 128), 128)
+            hidden[s, :, to] = jnp.where(low_half, dv[0], dv[1]).astype(BF16)
+            return c
+
+        lax.fori_loop(0, pairs, pair, 0)
+        stack_tables(aid)
+        d_v = hidden[s, :, 2 * hw:3 * hw]
+        br = nt(d_v, u_cat[:, 2 * hw:3 * hw])
+        mine_rk[s, RK[4]:RK[5], :] = br.T[2 * RANK:3 * RANK, :]
+        rk_copy(s, 4).start()
+        back_rank[s] = wide(br, 64)
+        pack(2, s, 512, nn(rank_t[s, 2 * RANK:3 * RANK, :], d_v))
+        hosted(s, 0, lambda: gather_begin(1))
+        hosted(s, 1, lambda: gather_late(0))
+        return carry
+
+    lax.fori_loop(0, 2, stage4, 0)
+
+    def stage4b(s, carry):
+        aid = ids[s]
 
         def pair(hp, c):
             at = pl.ds(pl.multiple_of(hp * 128, 128), 128)
@@ -571,43 +613,38 @@
             v2 = qkv[s, 2, :, at]
             do2 = hidden[s, :, pl.ds(pl.multiple_of(3 * hw + hp * 128, 128), 128)]
             k2t = k2.T
-            zero = jnp.zeros_like(k2)
-            dk, dv = [], []
+            dk = []
             for j in range(2):
                 mine = low_half if j == 0 else jnp.logical_not(low_half)
                 h = 2 * hp + j
-                st = nt(jnp.where(mine, k2, zero), q2) + bias[s]
-                pt = jnp.exp(st - lse[s, pl.ds(h, 1), :])
-                dpt = nt(jnp.where(mine, v2, zero), do2)
-                dst = (pt * (dpt - drow[pl.ds(h, 1), :])).astype(BF16)
-                dv.append(nn(pt.astype(BF16), do2))
+                pt = ff[s, pl.ds(pl.multiple_of(hp * n, n), n), j * n:j * n + n].astype(F32)
+                dpt = nt(jnp.where(mine, v2, jnp.zeros_like(v2)), do2)
+                dst = (pt * (dpt - drow[s, pl.ds(h, 1), :])).astype(BF16)
                 dk.append(nn(dst, q2))
                 dqt = nn(k2t[j * HEAD_WIDTH:(j + 1) * HEAD_WIDTH, :], dst) * 0.125
                 slope[s, pl.ds(pl.multiple_of(h * HEAD_WIDTH, HEAD_WIDTH), HEAD_WIDTH), 0:n] = dqt.astype(BF16)
-            to = pl.multiple_of(hp * 128, 128)
-            hidden[s, :, pl.ds(hw + to, 128)] = jnp.where(low_half, dk[0], dk[1]).astype(BF16)
-            hidden[s, :, pl.ds(2 * hw + to, 128)] = jnp.where(low_half, dv[0], dv[1]).astype(BF16)
-            between(s, hp)
+            to = pl.ds(pl.multiple_of(hw + hp * 128, 128), 128)
+            hidden[s, :, to] = jnp.where(low_half, dk[0], dk[1]).astype(BF16)
+            for (s_, hp_), f in plan.items():
+                hosted(4 * s + hp, 4 * s_ + hp_, f)
             return c
 
         lax.fori_loop(0, pairs, pair, 0)
         hidden[s, :, 0:hw] = slope[s, 0:hw, 0:n].T
         stack_tables(aid)
-        br = nt(hidden[s, :, 0:3 * hw], u_cat[...])
-        mine_rk[s, 3 * RANK:6 * RANK, :] = br.T[0:3 * RANK, :]
+        br = nt(hidden[s, :, 0:2 * hw], u_cat[:, 0:2 * hw])
+        mine_rk[s, RK[3]:RK[4], :] = br.T[0:2 * RANK, :]
         rk_copy(s, 3).start()
-        back_rank[s] = wide(br, 64)
-        for p in range(3):
+        back_rank[s] += wide(br, 64)
+        for p in range(2):
             pack(
                 3, s, 512 * p, nn(rank_t[s, RANK * p:RANK * p + RANK, :], hidden[s, :, hw * p:hw * p + hw])
             )
-        t_d = term(rank_sum(s, 3, 3 * RANK), x[s, :, half])
-        for p in range(3):
-            pack(3, s, 1536 + 512 * p, t_d[RANK * p:RANK * p + RANK, :])
-        scatter(3, s)
+        hosted(s, 0, lambda: gather_begin(2))
         return carry
 
-    lax.fori_loop(0, 2, stage4, 0)
+    plan = {(0, 0): lambda: finish(2, 1), (0, 1): lambda: gather_middle(1), (1, 0): lambda: finish(3, 0), (1, 2): lambda: gather_late(1)}
+    lax.fori_loop(0, 2, stage4b, 0)
 
     def project_back(s, carry):
         stack_tables(ids[s])
@@ -617,8 +654,13 @@
         send(s)
         return carry
 
-    lax.fori_loop(0, 2, project_back, 0)
-    gather_middle(2)
+    def back_step(s, carry):
+        project_back(s, carry)
+        hosted(s, 0, lambda: finish(3, 1))
+        hosted(s, 0, lambda: gather_middle(2))
+        return carry
+
+    lax.fori_loop(0, 2, back_step, 0)
 
     def stage5(s):
         exchange(s).wait()
@@ -635,7 +677,8 @@
     gather_begin(3)
     gather_late(2)
     stage5(0)
-    gather_step(3, 1)
+    gather_onward(3, 0)
+    gather_unit(3, 1)
     stage5(1)
     for g in (0, 1, 2):
         gather_close(g)
@@ -696,12 +739,15 @@
     for i in (2, 5):
         loads[i].wait()
     fill(2, 0, od, 4, False)
-    fill(2, 512, ou, 4, True)
+    fill(2, 512, vu, 4, False)
+    fill(2, 1024, ou, 4, True)
+    fill(2, 1536, vd, 4, True)
     for i in (3, 6):
         loads[i].wait()
-    for p, (up, down) in enumerate(((qu, qd), (ku, kd), (vu, vd))):
-        fill(3, 512 * p, up, 4, False)
-        fill(3, 1536 + 512 * p, down, 4, True)
+    fill(3, 0, qu, 4, False)
+    fill(3, 512, ku, 4, False)
+    fill(3, 1024, qd, 4, True)
+    fill(3, 1536, kd, 4, True)
     for i in range(2):
         loads[7 + i].wait()
         store(src_v[7 + i], i)
@@ -750,8 +796,7 @@
             pltpu.VMEM((s, n, d), BF16),
             pltpu.VMEM((d, 3 * hw), BF16),
             pltpu.VMEM((hw, d), BF16),
-            pltpu.VMEM((d, f), BF16),
-            pltpu.VMEM((f, d), BF16),
+            pltpu.VMEM((2, f, d), BF16),
             pltpu.VMEM((3, 8, RANK, d), BF16),
             pltpu.VMEM((3, 8, RANK, hw), BF16),
             pltpu.VMEM((s, 3, n, hw), BF16),
@@ -772,7 +817,7 @@
             pltpu.VMEM((n, 128), F32),
             pltpu.VMEM((s, 3 * RANK, n), BF16),
             pltpu.VMEM((s, RANK, n), BF16),
-            pltpu.VMEM((RANK, n), F32),
+            pltpu.VMEM((s, RANK, n), F32),
             pltpu.VMEM((s, 6 * RANK, n), F32),
             pltpu.VMEM((s, 6 * RANK, n), F32),
             pltpu.VMEM((s, n, d), BF16),
@@ -781,13 +826,12 @@
             *(pltpu.VMEM((s, GROUP, 8, w), F32) for w in LANES),
             *(pltpu.VMEM((GROUP, s, 8, w), F32) for w in LANES),
             *(pltpu.VMEM((8, 8, w), F32) for w in LANES),
-            pltpu.SemaphoreType.DMA((21,)),
+            pltpu.SemaphoreType.DMA((22,)),
             pltpu.SemaphoreType.DMA((2,)),
             pltpu.SemaphoreType.DMA((2,)),
             pltpu.SemaphoreType.DMA((2,)),
             pltpu.SemaphoreType.REGULAR((2,)),
-            pltpu.SemaphoreType.DMA((2, 4)),
-            pltpu.SemaphoreType.DMA((2, 4)),
+            *(pltpu.SemaphoreType.DMA((2, 5)),) * 2,
             pltpu.SemaphoreType.DMA((GROUP,)),
             pltpu.SemaphoreType.DMA((GROUP,)),
             *(pltpu.SemaphoreType.DMA((len(LANES), 2, GROUP)),) * 2,

time: 142 us -> 136 us (0.958)
  Pallas kernels: 141 us -> 135 us
    pallas_call x1, Pallas kernels: 134 us -> 128 us  [layer(): pl.pallas_call(layer_kernel, out_shape=(sds((s, n, d), BF16), sds((s, n,...]
where the time goes in v5:
time: 136 us
  Pallas kernels  135 us (99%)
    pallas_call x1, Pallas kernels, layer(): pl.pallas_call(layer_kernel, out_shape=(sds((s, n, d), BF16), sds((s, n,...  128 us
    pallas_call x1, Pallas kernels, place(): pl.pallas_call(place_kernel, out_shape=[jax.ShapeDtypeStruct((s, n, d), B...  7.19 us

profile of v5, /device:TPU:0, one launch (start us, length us, event | category | flops | bytes accessed | tf_op | source)
XLA Modules:
  0.0 135.7 jit_solution(7148644875192398866)
XLA Ops:
  0.7 127.6 %shard_map.353 = (bf16[2,512,1024]{2,1,0:T(8,128)(2,1)}, bf16[2,512,1024]{2,1,0:T(8,128)(2,1)}, f32[16,8,8,256]{3,2,1,0:T(8,128)}, f32[16,8,8,384]{3,2,1,0:T(8,1...) custom-call(s32[2]{0:T(128)} %ids.1, ...), custom_call_target="tpu_custom_call" | custom-call | tf_op jit(solution)/shard_map/pallas_call | solution.py:784
  128.3 7.2 %shard_map.354 = (bf16[2,512,1024]{2,1,0:T(8,128)(2,1)}, bf16[2,512,1024]{2,1,0:T(8,128)(2,1)}, f32[8,16,1024]{2,1,0:T(8,128)}, f32[8,16,512]{2,1,0:T(8,128)}, f...) custom-call(f32[16,8,8,256]{3,2,1,0:T(8,128)} %get-tuple-element.37., ...), custom_call_target="tpu_custom_call" | custom-call | tf_op jit(solution)/shard_map/pallas_call | solution.py:763

commit v6 on v5

--- a/solution.py
+++ b/solution.py
@@ -11,7 +11,7 @@
 F32 = jnp.float32
 BF16 = jnp.bfloat16
 EPS = 1e-05
-ROWS = 128
+ROWS = 256
 GROUP = 16
 LANES = (256, 384, 256, 256)
 GROUPS = range(len(LANES))

time: 136 us -> 136 us (level)
  no operation moved by 1% of the time
where the time goes in v6:
time: 136 us
  Pallas kernels  135 us (99%)
    pallas_call x1, Pallas kernels, layer(): pl.pallas_call(layer_kernel, out_shape=(sds((s, n, d), BF16), sds((s, n,...  128 us
    pallas_call x1, Pallas kernels, place(): pl.pallas_call(place_kernel, out_shape=[jax.ShapeDtypeStruct((s, n, d), B...  7.19 us

profile of v6, /device:TPU:0, one launch (start us, length us, event | category | flops | bytes accessed | tf_op | source)
XLA Modules:
  0.0 135.6 jit_solution(3716660131636313981)
XLA Ops:
  0.7 127.5 %shard_map.353 = (bf16[2,512,1024]{2,1,0:T(8,128)(2,1)}, bf16[2,512,1024]{2,1,0:T(8,128)(2,1)}, f32[16,8,8,256]{3,2,1,0:T(8,128)}, f32[16,8,8,384]{3,2,1,0:T(8,1...) custom-call(s32[2]{0:T(128)} %ids.1, ...), custom_call_target="tpu_custom_call" | custom-call | tf_op jit(solution)/shard_map/pallas_call | solution.py:784
  128.2 7.2 %shard_map.354 = (bf16[2,512,1024]{2,1,0:T(8,128)(2,1)}, bf16[2,512,1024]{2,1,0:T(8,128)(2,1)}, f32[8,16,1024]{2,1,0:T(8,128)}, f32[8,16,512]{2,1,0:T(8,128)}, f...) custom-call(f32[16,8,8,256]{3,2,1,0:T(8,128)} %get-tuple-element.37., ...), custom_call_target="tpu_custom_call" | custom-call | tf_op jit(solution)/shard_map/pallas_call | solution.py:763
